TPU v7x, 32 devices: a whole 2x2x4 slice. The times are simulated.
32 devices in a mesh: fsdp: 2 (over y), ctx: 8 (over z, x), tp: 2 (over core).
Axes of the slice: x: 2, y: 2, z: 4, core: 2. Of those that a mesh axis runs over, the one named last changes fastest.
Arguments:
- hidden_in: bfloat16 [2, 2048, 1024], P('fsdp', 'ctx'), may hold values from -6 to 6
- segments: int32 [2, 2048], P('fsdp', 'ctx'), may hold values from 0 to 2, never falling along the last dimension, each value on 1 to 1024 neighbouring positions
- cotangent: bfloat16 [2, 2048, 1024], P('fsdp', 'ctx'), may hold values from -6 to 6
- norm_gain: float32 [2, 1024], P('fsdp'), may hold values from 0.5 to 1.5
- in_proj: bfloat16 [2, 1024, 2, 2048], P(None, ('fsdp', 'ctx'), None, 'tp'), may hold values from -0.1875 to 0.1875
- step_proj: bfloat16 [2, 1024, 32], P(None, ('fsdp', 'ctx'), 'tp'), may hold values from -0.1875 to 0.1875
- state_proj: bfloat16 [2, 1024, 256], P(None, ('fsdp', 'ctx')), may hold values from -0.1875 to 0.1875
- out_proj: bfloat16 [2, 1024, 2048], P(None, ('fsdp', 'ctx'), 'tp'), may hold values from -0.125 to 0.125
- conv_inner: float32 [2, 4, 2048], P('fsdp', None, 'tp'), may hold values from -3 to 3
- inner_bias: float32 [2, 2048], P('fsdp', 'tp'), may hold values from -0.5 to 0.5
- conv_state: float32 [2, 4, 256], P('fsdp'), may hold values from -3 to 3
- state_bias: float32 [2, 256], P('fsdp'), may hold values from -0.5 to 0.5
- step_bias: float32 [2, 32], P('fsdp', 'tp'), may hold values from -5 to 0
- decay_log: float32 [2, 32], P('fsdp', 'tp'), may hold values from -6.9 to -1.9
- skip_scale: float32 [2, 32], P('fsdp', 'tp'), may hold values from 0.5 to 2
- gate_gain: float32 [2, 2048], P('fsdp', 'tp'), may hold values from 0.5 to 1.5
Outputs:
- hidden_out: bfloat16 [2, 2048, 1024], P('fsdp', 'ctx')
- hidden_grad: float32 [2, 2048, 1024], P('fsdp', 'ctx')
- grad_norm_gain: float32 [2, 1024], P('fsdp')
- grad_in_proj: float32 [2, 1024, 2, 2048], P(None, ('fsdp', 'ctx'), None, 'tp')
- grad_step_proj: float32 [2, 1024, 32], P(None, ('fsdp', 'ctx'), 'tp')
- grad_state_proj: float32 [2, 1024, 256], P(None, ('fsdp', 'ctx'))
- grad_out_proj: float32 [2, 1024, 2048], P(None, ('fsdp', 'ctx'), 'tp')
- grad_conv_inner: float32 [2, 4, 2048], P('fsdp', None, 'tp')
- grad_inner_bias: float32 [2, 2048], P('fsdp', 'tp')
- grad_conv_state: float32 [2, 4, 256], P('fsdp')
- grad_state_bias: float32 [2, 256], P('fsdp')
- grad_step_bias: float32 [2, 32], P('fsdp', 'tp')
- grad_decay_log: float32 [2, 32], P('fsdp', 'tp')
- grad_skip_scale: float32 [2, 32], P('fsdp', 'tp')
- grad_gate_gain: float32 [2, 2048], P('fsdp', 'tp')
Inputs may be any that keep to these rules, and one draw needn't show every extreme that they name: `segments`: in each row the segment numbers start at 0, never fall and take every value up to 2; one packed sequence has exactly 1024 positions and none has more.
All inputs are finite; a program needn't handle non-finite values.
Results may differ from a plain program's by a relative error of at most 0.02.
The roundings to bfloat16 on the way count: a program that leaves them out, or rounds other values in their place, can miss the bound.
Values may be sent and summed in bfloat16 or wider, within the bound.
No kernel may reach another device: no remote copies, remote signals or barrier semaphores. Data moves between devices by JAX's collectives and lax.ppermute only.
A program may use at most 320 MiB of HBM per device.

v0:
```python
import jax
import jax.numpy as jnp
from jax import lax
from jax.sharding import PartitionSpec as P

INNER = 2048
BLOCK = 64


EPSILON = 1e-05
HIGHEST = lax.Precision.HIGHEST


def passed_along(block, axis, distance):
    devices = range(lax.axis_size(axis))
    route = [(i - distance, i) for i in devices if i - distance in devices]
    return lax.ppermute(block, axis, route)


def prefix_2(part, axis, combine, identity):
    place = lax.axis_index(axis)
    gathered = jax.tree.map(lambda a: lax.all_gather(a, axis), part)
    state = jax.tree.map(lambda a, e: jnp.zeros_like(a) + jnp.asarray(e, a.dtype), part, identity)

    def one(lap, state):
        return combine(
            state, jax.tree.map(lambda a: lax.dynamic_index_in_dim(a, lap, 0, False), gathered)
        )

    return lax.fori_loop(0, place, one, state)


def carried_in_2(x, axis, combine, identity):
    peers, place = (lax.axis_size(axis), lax.axis_index(axis))
    everything = jax.tree.map(
        lambda part, kind: lax.all_gather(part.astype(kind), axis),
        x,
        jax.tree.map(lambda a: jnp.bfloat16 if a.dtype == jnp.float32 else a.dtype, x),
    )
    start = jax.tree.map(
        lambda part, zero: jnp.broadcast_to(jnp.asarray(zero, part.dtype), part.shape), x, identity
    )

    def lap(k, before):
        at = peers - 1 - k
        reached = at > place
        new = combine(
            before, jax.tree.map(lambda part, own: part[at].astype(own.dtype), everything, x)
        )
        return jax.tree.map(lambda a, b: jnp.where(reached, a, b), new, before)

    return lax.fori_loop(0, peers, lap, start)


def matmul(former, latter):
    return jnp.dot(former, latter, preferred_element_type=jnp.float32)


def matmul_tn(former, latter):
    return lax.dot_general(
        former, latter, (((0,), (0,)), ((), ())), preferred_element_type=jnp.float32
    )


def matmul_nt(former, latter):
    return lax.dot_general(
        former, latter, (((1,), (1,)), ((), ())), preferred_element_type=jnp.float32
    )


def rms_norm(residual, scaling):
    return (
        residual
        * lax.rsqrt(jnp.mean(residual * residual, axis=1, keepdims=True) + EPSILON)
        * scaling[None, :]
    )


def gate_apply(mixed_all, gate_pre):
    return mixed_all * jax.nn.silu(gate_pre)


def causal_conv(padded, labels, kernel, offset):
    length = padded.shape[0] - kernel.shape[0] + 1
    current = labels[kernel.shape[0] - 1 :]
    result = jnp.zeros((length, padded.shape[1]), jnp.float32) + offset[None, :]
    for lag_index in range(kernel.shape[0]):
        matched = (labels[lag_index : lag_index + length] == current).astype(jnp.float32)
        result = (
            result
            + kernel[lag_index][None, :] * padded[lag_index : lag_index + length] * matched[:, None]
        )
    return result


def block_terms(values, write_map, read_map, step_size, decay_rate, labels, before):
    logdecay = step_size * decay_rate[None, :]
    cumulative = jnp.cumsum(logdecay, axis=0)
    position = jnp.arange(values.shape[0])
    visible = (position[:, None] >= position[None, :]) & (labels[:, None] == labels[None, :])
    spread = cumulative[:, None, :] - cumulative[None, :, :]
    kernels = jnp.exp(jnp.where(visible[:, :, None], spread, -1e30))
    affinity = jnp.dot(read_map, write_map.T, precision=HIGHEST)
    weights = affinity[:, :, None] * kernels * step_size[None, :, :]
    within = jnp.einsum("tsh,shp->thp", weights, values, precision=HIGHEST)
    closing = labels[-1]
    ending = (
        jnp.exp(cumulative[-1][None, :] - cumulative)
        * (labels == closing).astype(jnp.float32)[:, None]
        * step_size
    )
    produced = jnp.einsum("sh,shp,sn->hpn", ending, values, write_map, precision=HIGHEST)
    inflow = jnp.exp(cumulative) * (labels == before).astype(jnp.float32)[:, None]
    passing = jnp.exp(cumulative[-1]) * (closing == before).astype(jnp.float32)
    return (within, produced, inflow, passing)


def duality_core(
    values, write_map, read_map, step_pre, step_bias, decay_log, skip_scale, labels, incoming
):
    tokens, head_count, head_size = values.shape
    state_size = write_map.shape[1]
    blocks = tokens // BLOCK
    step_size = jax.nn.softplus(step_pre + step_bias[None, :])
    decay_rate = -jnp.exp(decay_log)
    part_values = values.reshape(blocks, BLOCK, head_count, head_size)
    part_write = write_map.reshape(blocks, BLOCK, state_size)
    part_read = read_map.reshape(blocks, BLOCK, state_size)
    part_step = step_size.reshape(blocks, BLOCK, head_count)
    part_labels = labels.reshape(blocks, BLOCK)
    befores = jnp.concatenate([jnp.reshape(incoming, (1,)), part_labels[:-1, -1]], axis=0)

    def one_block(pieces):
        return block_terms(
            pieces[0], pieces[1], pieces[2], pieces[3], decay_rate, pieces[4], pieces[5]
        )

    within, produced, inflow, passing = lax.map(
        one_block, (part_values, part_write, part_read, part_step, part_labels, befores)
    )

    def advance(carried_in, pieces):
        memory, factor = carried_in
        return (
            (pieces[1][:, None, None] * memory + pieces[0], factor * pieces[1]),
            (memory, factor),
        )

    initial = (
        jnp.zeros((head_count, head_size, state_size), jnp.float32),
        jnp.ones((head_count,), jnp.float32),
    )
    (closing, total_decay), (starting, leading) = lax.scan(advance, initial, (produced, passing))
    inside = (
        within
        + inflow[..., None] * jnp.einsum("ctn,chpn->cthp", part_read, starting, precision=HIGHEST)
        + skip_scale[None, None, :, None] * part_values
    )
    return (inside, inflow, leading, total_decay, closing)


def carry_term(read_map, inflow, leading, incoming_state):
    blocks, length, head_count = inflow.shape
    part_read = read_map.reshape(blocks, length, read_map.shape[1])
    starting = leading[:, :, None, None] * incoming_state[None]
    return inflow[..., None] * jnp.einsum("ctn,chpn->cthp", part_read, starting, precision=HIGHEST)


def compose(earlier, later):
    return (earlier[0] * later[0], later[0][:, None, None] * earlier[1] + later[1])


def fetch_weights(ordinal, in_proj, step_proj, state_proj, out_proj):
    return (
        lax.all_gather(in_proj[ordinal], ("fsdp", "ctx"), axis=0, tiled=True),
        lax.all_gather(step_proj[ordinal], ("fsdp", "ctx"), axis=0, tiled=True),
        lax.all_gather(state_proj[ordinal], ("fsdp", "ctx"), axis=0, tiled=True),
        lax.all_gather(out_proj[ordinal], ("fsdp", "ctx"), axis=0, tiled=True),
    )


def layer_forward(residual, labels, padded_labels, incoming, weights, params):
    weight_in, weight_step, weight_state, weight_out = weights
    prenorm, kernel, offset, step_bias, decay_log, skip_scale, gate_gain = params
    tokens, model_width = residual.shape
    margin = kernel.shape[0] - 1
    prenormed, norm_pull = jax.vjp(rms_norm, residual, prenorm)
    normed = prenormed.astype(jnp.bfloat16)
    local_inner = weight_in.shape[2]
    projected = matmul(normed, weight_in.reshape(model_width, 2 * local_inner))
    gate_pre = projected[:, :local_inner]
    step_pre = matmul(normed, weight_step)
    state_pre = matmul(normed, weight_state)
    joined = jnp.concatenate([projected[:, local_inner:], state_pre], axis=1)
    arriving = passed_along(joined[tokens - margin :], "ctx", 1)
    padded = jnp.concatenate([arriving, joined], axis=0)

    def convolve(padded_rows, taps, biases):
        return jax.nn.silu(causal_conv(padded_rows, padded_labels, taps, biases))

    active, conv_pull = jax.vjp(convolve, padded, kernel, offset)
    head_count = step_pre.shape[1]
    state_size = state_pre.shape[1] // 2
    values = active[:, :local_inner].reshape(tokens, head_count, local_inner // head_count)
    write_map = active[:, local_inner : local_inner + state_size]
    read_map = active[:, local_inner + state_size :]

    def core_local(values, write_map, read_map, step_pre, step_bias, decay_log, skip_scale):
        return duality_core(
            values,
            write_map,
            read_map,
            step_pre,
            step_bias,
            decay_log,
            skip_scale,
            labels,
            incoming,
        )

    core_out, core_pull = jax.vjp(
        core_local, values, write_map, read_map, step_pre, step_bias, decay_log, skip_scale
    )
    inside, inflow, leading, total_decay, closing = core_out
    identity = (jnp.ones_like(total_decay), jnp.zeros_like(closing))
    prefix = prefix_2((total_decay, closing), "ctx", compose, identity)
    incoming_state = prefix[1]
    carried, term_pull = jax.vjp(carry_term, read_map, inflow, leading, incoming_state)
    mixed_all = (inside + carried).reshape(tokens, local_inner)
    gated_rows, gate_pull = jax.vjp(gate_apply, mixed_all, gate_pre)
    squares = lax.psum(jnp.sum(gated_rows * gated_rows, axis=1), "tp")
    scaling = lax.rsqrt(squares / INNER + EPSILON)
    branch = (gated_rows * scaling[:, None] * gate_gain[None, :]).astype(jnp.bfloat16)
    partial_out = matmul_nt(branch, weight_out)
    updated = residual + lax.psum(partial_out, "tp")
    saved = (
        normed,
        branch,
        gated_rows,
        scaling,
        norm_pull,
        conv_pull,
        core_pull,
        term_pull,
        gate_pull,
        incoming_state,
        total_decay,
    )
    return (updated, saved)


def layer_backward(upstream, saved, weights, params):
    weight_in, weight_step, weight_state, weight_out = weights
    gate_gain = params[6]
    (
        normed,
        branch,
        gated_rows,
        scaling,
        norm_pull,
        conv_pull,
        core_pull,
        term_pull,
        gate_pull,
        incoming_state,
        total_decay,
    ) = saved
    tokens, model_width = upstream.shape
    local_inner = weight_in.shape[2]
    head_count, head_size = (incoming_state.shape[0], incoming_state.shape[1])
    outward = upstream.astype(jnp.bfloat16)
    grad_out = matmul_tn(outward, branch)
    grad_branch = matmul(outward, weight_out)
    grad_gain = jnp.sum(grad_branch * gated_rows * scaling[:, None], axis=0)
    projection = lax.psum(jnp.sum(grad_branch * gate_gain[None, :] * gated_rows, axis=1), "tp")
    grad_gated = (
        grad_branch * gate_gain[None, :] * scaling[:, None]
        - gated_rows * (scaling * scaling * scaling * projection / INNER)[:, None]
    )
    grad_mixed, grad_gate_pre = gate_pull(grad_gated)
    grad_inside = grad_mixed.reshape(-1, BLOCK, head_count, head_size)
    read_term, grad_inflow, grad_leading, grad_incoming = term_pull(grad_inside)
    identity = (jnp.ones_like(total_decay), jnp.zeros_like(grad_incoming))
    adjoint = carried_in_2((total_decay, grad_incoming), "ctx", compose, identity)[1]
    grad_decay = jnp.sum(adjoint * incoming_state, axis=(1, 2))
    grad_values, grad_write, grad_read, grad_step_pre, grad_step_bias, grad_decay_log, grad_skip = (
        core_pull((grad_inside, grad_inflow, grad_leading, grad_decay, adjoint))
    )
    grad_shared = lax.psum(
        jnp.concatenate([grad_write, grad_read + read_term], axis=1).astype(jnp.bfloat16), "tp"
    ).astype(jnp.float32)
    grad_active = jnp.concatenate([grad_values.reshape(tokens, local_inner), grad_shared], axis=1)
    grad_padded, grad_kernel, grad_offset = conv_pull(grad_active)
    margin = grad_padded.shape[0] - tokens
    returned = passed_along(grad_padded[:margin], "ctx", -1)
    grad_joined = grad_padded[margin:] + jnp.concatenate(
        [jnp.zeros((tokens - margin, grad_padded.shape[1]), jnp.float32), returned], axis=0
    )
    grad_pre = jnp.concatenate([grad_gate_pre, grad_joined[:, :local_inner]], axis=1).astype(
        jnp.bfloat16
    )
    grad_step_round = grad_step_pre.astype(jnp.bfloat16)
    grad_state_round = grad_joined[:, local_inner:].astype(jnp.bfloat16)
    grad_in = matmul_tn(normed, grad_pre).reshape(weight_in.shape)
    grad_step = matmul_tn(normed, grad_step_round)
    grad_state = matmul_tn(normed, grad_state_round)
    partial_normed = matmul_nt(
        grad_pre, weight_in.reshape(model_width, 2 * local_inner)
    ) + matmul_nt(grad_step_round, weight_step)
    grad_normed = lax.psum(partial_normed.astype(jnp.bfloat16), "tp").astype(
        jnp.float32
    ) + matmul_nt(grad_state_round, weight_state)
    grad_residual, grad_prenorm = norm_pull(grad_normed)
    shards = (
        lax.psum_scatter(grad_in, ("fsdp", "ctx"), scatter_dimension=0, tiled=True),
        lax.psum_scatter(grad_step, ("fsdp", "ctx"), scatter_dimension=0, tiled=True),
        lax.psum_scatter(grad_state, ("fsdp", "ctx"), scatter_dimension=0, tiled=True),
        lax.psum_scatter(grad_out, ("fsdp", "ctx"), scatter_dimension=0, tiled=True),
    )
    mixer_grads = (
        grad_prenorm,
        grad_kernel,
        grad_offset,
        grad_step_bias,
        grad_decay_log,
        grad_skip,
        grad_gain,
    )
    return (upstream + grad_residual, shards, mixer_grads)


def on_device(
    hidden_in,
    segments,
    cotangent,
    norm_gain,
    in_proj,
    step_proj,
    state_proj,
    out_proj,
    conv_inner,
    inner_bias,
    conv_state,
    state_bias,
    step_bias,
    decay_log,
    skip_scale,
    gate_gain,
):
    layer_count = in_proj.shape[0]
    gathered = (
        lax.all_gather(norm_gain, "fsdp", axis=0, tiled=True),
        lax.all_gather(conv_inner, "fsdp", axis=0, tiled=True),
        lax.all_gather(inner_bias, "fsdp", axis=0, tiled=True),
        lax.all_gather(conv_state, "fsdp", axis=0, tiled=True),
        lax.all_gather(state_bias, "fsdp", axis=0, tiled=True),
        lax.all_gather(step_bias, "fsdp", axis=0, tiled=True),
        lax.all_gather(decay_log, "fsdp", axis=0, tiled=True),
        lax.all_gather(skip_scale, "fsdp", axis=0, tiled=True),
        lax.all_gather(gate_gain, "fsdp", axis=0, tiled=True),
    )
    labels = segments[0]
    margin = conv_inner.shape[1] - 1
    arrived = passed_along(labels[labels.shape[0] - margin :], "ctx", 1)
    padded_labels = jnp.concatenate([arrived, labels], axis=0)
    incoming = arrived[margin - 1]
    local_inner = in_proj.shape[3]
    residual = hidden_in[0].astype(jnp.float32)
    kept = []
    records = []
    layer_params = []
    for ordinal in range(layer_count):
        params = (
            gathered[0][ordinal],
            jnp.concatenate([gathered[1][ordinal], gathered[3][ordinal]], axis=1),
            jnp.concatenate([gathered[2][ordinal], gathered[4][ordinal]], axis=0),
            gathered[5][ordinal],
            gathered[6][ordinal],
            gathered[7][ordinal],
            gathered[8][ordinal],
        )
        weights = fetch_weights(ordinal, in_proj, step_proj, state_proj, out_proj)
        residual, saved = layer_forward(residual, labels, padded_labels, incoming, weights, params)
        kept.append(weights)
        records.append(saved)
        layer_params.append(params)
    hidden_out = residual.astype(jnp.bfloat16)[None]
    upstream = cotangent[0].astype(jnp.float32)
    weight_shards = [None] * layer_count
    mixer_lists = [None] * layer_count
    for ordinal in reversed(range(layer_count)):
        weights = fetch_weights(ordinal, in_proj, step_proj, state_proj, out_proj)
        upstream, shards, mixer_grads = layer_backward(
            upstream, records[ordinal], weights, layer_params[ordinal]
        )
        weight_shards[ordinal] = shards
        mixer_lists[ordinal] = mixer_grads
    stacked = tuple(
        (
            jnp.stack([weight_shards[ordinal][member] for ordinal in range(layer_count)], axis=0)
            for member in range(4)
        )
    )
    small_stack = [
        jnp.stack([mixer_lists[ordinal][member] for ordinal in range(layer_count)], axis=0)
        for member in range(7)
    ]
    kernels_all = small_stack[1]
    offsets_all = small_stack[2]
    summed = lax.psum(
        (
            small_stack[0],
            kernels_all[:, :, :local_inner],
            offsets_all[:, :local_inner],
            kernels_all[:, :, local_inner:],
            offsets_all[:, local_inner:],
            small_stack[3],
            small_stack[4],
            small_stack[5],
            small_stack[6],
        ),
        ("fsdp", "ctx"),
    )
    per_shard = layer_count // lax.axis_size("fsdp")
    first_layer = lax.axis_index("fsdp") * per_shard
    owned = tuple(
        (lax.dynamic_slice_in_dim(summed_item, first_layer, per_shard, 0) for summed_item in summed)
    )
    return (hidden_out, upstream[None], owned[0]) + stacked + owned[1:]


def solution(mesh):
    placed = (
        P("fsdp", "ctx", None),
        P("fsdp", "ctx"),
        P("fsdp", "ctx", None),
        P("fsdp", None),
        P(None, ("fsdp", "ctx"), None, "tp"),
        P(None, ("fsdp", "ctx"), "tp"),
        P(None, ("fsdp", "ctx"), None),
        P(None, ("fsdp", "ctx"), "tp"),
        P("fsdp", None, "tp"),
        P("fsdp", "tp"),
        P("fsdp", None, None),
        P("fsdp", None),
        P("fsdp", "tp"),
        P("fsdp", "tp"),
        P("fsdp", "tp"),
        P("fsdp", "tp"),
    )
    return jax.shard_map(
        on_device,
        mesh=mesh,
        in_specs=placed,
        out_specs=(
            P("fsdp", "ctx", None),
            P("fsdp", "ctx", None),
            P("fsdp", None),
            P(None, ("fsdp", "ctx"), None, "tp"),
            P(None, ("fsdp", "ctx"), "tp"),
            P(None, ("fsdp", "ctx"), None),
            P(None, ("fsdp", "ctx"), "tp"),
            P("fsdp", None, "tp"),
            P("fsdp", "tp"),
            P("fsdp", None, None),
            P("fsdp", None),
            P("fsdp", "tp"),
            P("fsdp", "tp"),
            P("fsdp", "tp"),
            P("fsdp", "tp"),
        ),
        check_vma=False,
    )
```

profile of v0, /device:TPU:0, one launch (start us, length us, event | category | flops | bytes accessed | tf_op | source)
XLA Modules:
  0.0 2419.0 jit_solution(3061499529333478959)
XLA Ops:
  10.4 4.9 collective-permute-start.1
  15.2 4.4 all-gather.19
  19.6 4.4 all-gather.20
  25.4 43.2 %all-gather.2 = bf16[1,1024,16]{2,0,1:T(2,128)(2,1)S(1)} all-gather(bf16[1,64,16]{2,0,1:T(2,128)(2,1)S(1)} %copy.533), channel_id=4, replica_groups=mesh['fsdp'=2,'ctx'=8,'tp'=2] {'fsdp','ctx'}, dimensions={1}, use_global_device_ids=true | all-gather | bytes 34816 | tf_op jit(solution)/shard_map/all_gather | solution.py:176
  68.8 4.6 all-gather.18
  78.2 4.4 all-gather.17
  82.6 4.3 all_gather.106
  87.0 4.3 all-gather.16
  91.3 4.5 all_gather.105
  100.3 39.1 %all-gather.1 = bf16[1,1024,256]{2,1,0:T(8,128)(2,1)S(1)} all-gather(bf16[1,64,256]{2,1,0:T(8,128)(2,1)S(1)} %get-tuple-element.4291), channel_id=3, replica_groups=mesh['fsdp'=2,'ctx'=8,'tp'=2] {'fsdp','ctx'}, dimensions={1}, use_global_device_ids=true | all-gather | bytes 557056 | tf_op jit(solution)/shard_map/all_gather | solution.py:177
  177.7 108.4 %while.284 = (s32[]{:T(128)}, f32[4,64,16,64]{1,3,2,0:T(8,128)}, f32[4,16,64,128]{3,2,1,0:T(8,128)}, f32[4,64,16]{1,2,0:T(8,128)}, f32[4,16]{1,0:T(4,128)}, /*in...) while((s32[]{:T(128)}, f32[4,64,16,64]{1,3,2,0:T(8,128)}, ...), condition=%wide.region_3.5_spmd.clone, body=%wide.region_1.4_spmd.clone.sunk | while | flops 158027280 | bytes 5236955 | solution.py:138
  287.8 8.4 while.286
  299.4 4.2 all-gather.21
  304.8 4.4 all-gather.22
  309.9 19.8 all-reduce.22
  329.9 4.7 fusion.410
  334.6 33.9 %all-gather.34.cloned.1.call-done = f32[128,64,128]{2,1,0:T(8,128)} async-done(((f32[16,64,128]{2,1,0:T(8,128)}), f32[128,64,128]{2,1,0:T(8,128)}) %all-gather.34.cloned.1.call-update) | async-done | bytes 4194320 | tf_op jit(solution)/shard_map/all_gather | solution.py:22
  371.8 4.0 multiply_add_fusion.3
  385.5 45.4 %all-gather.36.cloned.1.call-done = bf16[1,1024,1024]{2,1,0:T(8,128)(2,1)} async-done(((bf16[1,64,1024]{2,1,0:T(8,128)(2,1)}), bf16[1,1024,1024]{2,1,0:T(8,128)(2,1)}) %all-gather.36.cloned.1.call-update) | async-done | bytes 2097168 | tf_op jit(solution)/shard_map/all_gather | solution.py:178
  434.4 43.2 %all-gather.8 = bf16[1,1024,16]{2,0,1:T(2,128)(2,1)S(1)} all-gather(bf16[1,64,16]{2,0,1:T(2,128)(2,1)S(1)} %copy.535), channel_id=10, replica_groups=mesh['fsdp'=2,'ctx'=8,'tp'=2] {'fsdp','ctx'}, dimensions={1}, use_global_device_ids=true | all-gather | bytes 34816 | tf_op jit(solution)/shard_map/all_gather | solution.py:176
  478.1 42.4 %all-gather.7 = bf16[1,1024,256]{2,1,0:T(8,128)(2,1)S(1)} all-gather(bf16[1,64,256]{2,1,0:T(8,128)(2,1)S(1)} %copy-done.96), channel_id=9, replica_groups=mesh['fsdp'=2,'ctx'=8,'tp'=2] {'fsdp','ctx'}, dimensions={1}, use_global_device_ids=true | all-gather | bytes 557056 | tf_op jit(solution)/shard_map/all_gather | solution.py:177
  520.5 5.8 copy.593
  526.3 12.8 all-reduce.36.cloned.1.call-done
  544.3 4.1 collective-permute-start.2
  570.3 64.6 %while.285 = (s32[]{:T(128)}, f32[4,64,16,64]{1,3,2,0:T(8,128)}, f32[4,16,64,128]{3,2,1,0:T(8,128)}, f32[4,64,16]{1,2,0:T(8,128)S(1)}, f32[4,16]{1,0:T(4,128)S(1...) while((s32[]{:T(128)}, f32[4,64,16,64]{1,3,2,0:T(8,128)}, ...), condition=%wide.region_14.16_spmd.clone, body=%wide.region_12.15_spmd.clone.sunk | while | flops 158027280 | bytes 5321707 | solution.py:138
  636.6 8.4 while.287
  646.9 22.7 all-reduce.23
  669.7 4.7 fusion.412
  674.3 46.3 %all-gather.40.cloned.1.call-done = f32[128,64,128]{2,1,0:T(8,128)} async-done(((f32[16,64,128]{2,1,0:T(8,128)}), f32[128,64,128]{2,1,0:T(8,128)}) %all-gather.40.cloned.1.call-update) | async-done | bytes 4194320 | tf_op jit(solution)/shard_map/all_gather | solution.py:22
  724.2 4.0 multiply_add_fusion.2
  737.8 45.2 %all-gather.42.cloned.1.call-done = bf16[1,1024,1024]{2,1,0:T(8,128)(2,1)} async-done(((bf16[1,64,1024]{2,1,0:T(8,128)(2,1)}), bf16[1,1024,1024]{2,1,0:T(8,128)(2,1)}) %all-gather.42.cloned.1.call-update) | async-done | bytes 2097168 | tf_op jit(solution)/shard_map/all_gather | solution.py:178
  783.0 4.2 multiply_reduce_fusion.20
  789.7 4.3 multiply_reduce_fusion.22
  799.0 4.3 multiply_reduce_fusion.10
  804.6 20.7 all-reduce.27
  829.7 21.7 all-gather.44.cloned.1.call-done
  851.4 14.4 while.288
  867.7 14.9 while.282
  885.5 139.7 %while.289 = (s32[]{:T(128)}, f32[16]{0:T(128)}, f32[4,64,16,64]{1,3,2,0:T(8,128)}, bf16[4,64,128]{2,1,0:T(8,128)(2,1)}, f32[4,64,128]{2,1,0:T(8,128)}, /*index=...) while((s32[]{:T(128)}, f32[16]{0:T(128)}, ...), condition=%wide.region_42.44_spmd.clone, body=%wide.region_34.43_spmd.clone.sunk | while | flops 315574304 | bytes 10803031 | solution.py:138
  1036.7 5.2 fusion.260
  1048.5 14.6 all-reduce.40.cloned.1.call-done
  1080.0 16.2 all-reduce.42.cloned.1.call-done
  1099.3 20.4 all-reduce.38.cloned.1.call-done
  1137.9 4.3 multiply_reduce_fusion.6
  1146.2 46.4 %all-gather.46.cloned.1.call-done = bf16[128,64,128]{2,1,0:T(8,128)(2,1)} async-done(((bf16[16,64,128]{2,1,0:T(8,128)(2,1)}), bf16[128,64,128]{2,1,0:T(8,128)(2,1)}) %all-gather.46.cloned.1.call-update) | async-done | bytes 2097168 | tf_op jit(solution)/shard_map/all_gather | solution.py:36
  1192.6 9.1 while.290
  1203.6 14.7 while.283
  1221.3 135.9 %while.291 = (s32[]{:T(128)}, f32[16]{0:T(128)}, f32[4,64,16,64]{1,3,2,0:T(8,128)}, bf16[4,64,128]{2,1,0:T(8,128)(2,1)}, f32[4,64,128]{2,1,0:T(8,128)}, /*index=...) while((s32[]{:T(128)}, f32[16]{0:T(128)}, ...), condition=%wide.region_66.68_spmd.clone, body=%wide.region_58.67_spmd.clone.sunk | while | flops 315574304 | bytes 10803031 | solution.py:138
  1366.8 5.2 fusion.257
  1378.4 14.7 all-reduce.44.cloned.1.call-done
  1394.1 5.3 multiply_reduce_fusion.18
  1415.6 12.9 all-reduce.46.cloned.1.call-done
  1443.9 4.6 fusion.306
  1448.5 8.7 copy.456
  1461.0 4.8 fusion.309
  1465.8 43.7 %reduce-scatter.27.cloned.1.call-done = f32[64,16]{1,0:T(8,128)} async-done(((f32[1024,16]{1,0:T(8,128)}), f32[64,16]{1,0:T(8,128)}) %reduce-scatter.27.cloned.1.call-update) | async-done | bytes 4112
  1510.2 75.3 %reduce-scatter.25.cloned.1.call-done = f32[64,16]{1,0:T(8,128)} async-done(((f32[1024,16]{1,0:T(8,128)}), f32[64,16]{1,0:T(8,128)}) %reduce-scatter.25.cloned.1.call-update) | async-done | bytes 4112
  1588.2 110.2 %all-reduce.48.cloned.1.call-done = (f32[2,1024]{1,0:T(2,128)}, f32[2,4,1024]{2,1,0:T(4,128)}, f32[2,1024]{1,0:T(2,128)}, f32[2,4,256]{2,1,0:T(4,128)}, f32[2,25...) async-done(((f32[2,1024]{1,0:T(2,128)}, f32[2,4,1024]{2,1,0:T(4,128)}, f32[2,1024]{1,0:T(2,128)}, ...) | async-done | bytes 67984 | tf_op jit(solution)/shard_map/psum | solution.py:410
  1709.7 69.6 %reduce-scatter.19.cloned.1.call-done = f32[64,256]{1,0:T(8,128)} async-done(((f32[1024,256]{1,0:T(8,128)}), f32[64,256]{1,0:T(8,128)}) %reduce-scatter.19.cloned.1.call-update) | async-done | bytes 65552 | tf_op jit(solution)/shard_map/reduce_scatter | solution.py:317
  1779.3 77.4 %reduce-scatter.17.cloned.1.call-done = f32[64,256]{1,0:T(8,128)} async-done(((f32[1024,256]{1,0:T(8,128)}), f32[64,256]{1,0:T(8,128)}) %reduce-scatter.17.cloned.1.call-update) | async-done | bytes 65552 | tf_op jit(solution)/shard_map/reduce_scatter | solution.py:317
  1858.3 94.0 %reduce-scatter.23.cloned.1.call-done = f32[64,1024]{1,0:T(8,128)} async-done(((f32[1024,1024]{1,0:T(8,128)}), f32[64,1024]{1,0:T(8,128)}) %reduce-scatter.23.cloned.1.call-update) | async-done | bytes 262160 | tf_op jit(solution)/shard_map/reduce_scatter | solution.py:318
  1952.3 97.4 %reduce-scatter.21.cloned.1.call-done = f32[64,1024]{1,0:T(8,128)} async-done(((f32[1024,1024]{1,0:T(8,128)}), f32[64,1024]{1,0:T(8,128)}) %reduce-scatter.21.cloned.1.call-update) | async-done | bytes 262160 | tf_op jit(solution)/shard_map/reduce_scatter | solution.py:318
  2051.6 177.5 %reduce-scatter.15.cloned.1.call-done = f32[64,2,1024]{2,0,1:T(8,128)} async-done(((f32[1024,2,1024]{2,0,1:T(8,128)}), f32[64,2,1024]{2,0,1:T(8,128)}) %reduce-scatter.15.cloned.1.call-update) | async-done | bytes 524304 | tf_op jit(solution)/shard_map/reduce_scatter | solution.py:315
  2229.1 179.9 %reduce-scatter.13.cloned.1.call-done = f32[64,2,1024]{2,0,1:T(8,128)} async-done(((f32[1024,2,1024]{2,0,1:T(8,128)}), f32[64,2,1024]{2,0,1:T(8,128)}) %reduce-scatter.13.cloned.1.call-update) | async-done | bytes 524304 | tf_op jit(solution)/shard_map/reduce_scatter | solution.py:315
  (1467 shorter events, 779.9 us)
Async XLA Ops:
  7.2 69.7 %copy-start.184 = (s32[1,256]{1,0:T(1,128)S(1)}, s32[1,256]{1,0:T(1,128)}, u32[]{:S(2)}) copy-start(s32[1,256]{1,0:T(1,128)} %param.42) | copy-start | bytes 3076
  7.2 61.6 %copy-start.189 = (f32[1,1024]{1,0:T(1,128)S(1)}, f32[1,1024]{1,0:T(1,128)}, u32[]{:S(2)}) copy-start(f32[1,1024]{1,0:T(1,128)} %param.44) | copy-start | bytes 12292
  7.2 66.2 %copy-start.22 = (bf16[1,256,1024]{2,1,0:T(8,128)(2,1)S(1)}, bf16[1,256,1024]{2,1,0:T(8,128)(2,1)}, u32[]{:S(2)}) copy-start(bf16[1,256,1024]{2,1,0:T(8,128)(2,1)} %param.41) | copy-start | bytes 1572868
  7.2 71.0 %copy-start.200 = (f32[1,256]{1,0:T(1,128)S(1)}, f32[1,256]{1,0:T(1,128)}, u32[]{:S(2)}) copy-start(f32[1,256]{1,0:T(1,128)} %param.52) | copy-start | bytes 3076
  7.2 75.4 %copy-start.190 = (f32[1,4,256]{2,1,0:T(4,128)S(1)}, f32[1,4,256]{2,1,0:T(4,128)}, u32[]{:S(2)}) copy-start(f32[1,4,256]{2,1,0:T(4,128)} %param.51) | copy-start | bytes 12292
  7.2 79.7 %copy-start.191 = (f32[1,1024]{1,0:T(1,128)S(1)}, f32[1,1024]{1,0:T(1,128)}, u32[]{:S(2)}) copy-start(f32[1,1024]{1,0:T(1,128)} %param.50) | copy-start | bytes 12292
  7.2 84.1 %copy-start.162 = (f32[1,4,1024]{2,1,0:T(4,128)S(1)}, f32[1,4,1024]{2,1,0:T(4,128)}, u32[]{:S(2)}) copy-start(f32[1,4,1024]{2,1,0:T(4,128)} %param.49) | copy-start | bytes 49156
  7.3 92.4 %copy-start.122 = (bf16[2,64,256]{2,1,0:T(8,128)(2,1)S(1)}, bf16[2,64,256]{2,1,0:T(8,128)(2,1)}, u32[]{:S(2)}) copy-start(bf16[2,64,256]{2,1,0:T(8,128)(2,1)} %param.47) | copy-start | bytes 196612
  7.3 133.3 %all-gather.32.cloned.1.call-start = ((), (), s32[]{:S(2)}) async-start(), calls=%async_computation.20 | async-start | bytes 4456448 | tf_op jit(solution)/shard_map/all_gather | solution.py:175
  9.6 358.9 %all-gather.34.cloned.1.call-start = ((), (), s32[]{:S(2)}) async-start(), calls=%async_computation.21 | async-start | bytes 4718592 | tf_op jit(solution)/shard_map/all_gather | solution.py:22
  10.4 129.4 %collective-permute-start.1 = (s32[3]{0:T(128)S(1)}, s32[3]{0:T(128)S(1)}, u32[]{:S(2)}, u32[]{:S(2)}) collective-permute-start(s32[3]{0:T(128)S(1)} %slice_bitcast_fusion.12), channel_id=1, source_target_pairs={{0,2},{2,4},{4,6},{6,8},{8,10},{10,12},{12,14},{1,3},{3,5},{5,7},{... | collective-permute-start | bytes 44 | tf_op jit(solution)/shard_map/ppermute | solution.py:17
  24.0 75.1 %copy-start.193 = (f32[2,1,16]{2,1,0:T(1,128)}, f32[2,1,16]{2,1,0:T(1,128)S(1)}, u32[]{:S(2)}) copy-start(f32[2,1,16]{2,1,0:T(1,128)S(1)} %all-gather.20) | copy-start | bytes 388
  68.8 71.0 %copy-start.94 = (bf16[1,1024,16]{1,2,0:T(8,128)(2,1)}, bf16[1,1024,16]{1,2,0:T(8,128)(2,1)S(1)}, u32[]{:S(2)}) copy-start(bf16[1,1024,16]{1,2,0:T(8,128)(2,1)S(1)} %copy.392) | copy-start | bytes 98308
  74.1 70.1 %copy-start.145 = (f32[256]{0:T(256)}, f32[256]{0:T(256)S(1)}, u32[]{:S(2)}) copy-start(f32[256]{0:T(256)S(1)} %fusion.374) | copy-start | bytes 3076
  74.7 69.5 %copy-start.100 = (f32[1,1,1024]{2,1,0:T(1,128)}, f32[1,1,1024]{2,1,0:T(1,128)S(1)}, u32[]{:S(2)}) copy-start(f32[1,1,1024]{2,1,0:T(1,128)S(1)} %get-tuple-element.4303) | copy-start | bytes 12292
  97.0 54.0 %copy-start.107 = (f32[1280]{0:T(1024)}, f32[1280]{0:T(1024)S(1)}, u32[]{:S(2)}) copy-start(f32[1280]{0:T(1024)S(1)} %get-tuple-element.3790) | copy-start | bytes 15364
  97.1 54.0 %copy-start.109 = (f32[1280]{0:T(1024)}, f32[1280]{0:T(1024)S(1)}, u32[]{:S(2)}) copy-start(f32[1280]{0:T(1024)S(1)} %get-tuple-element.3791) | copy-start | bytes 15364
  97.1 54.0 %copy-start.111 = (f32[1280]{0:T(1024)}, f32[1280]{0:T(1024)S(1)}, u32[]{:S(2)}) copy-start(f32[1280]{0:T(1024)S(1)} %get-tuple-element.3792) | copy-start | bytes 15364
  97.1 54.0 %copy-start.113 = (f32[1280]{0:T(1024)}, f32[1280]{0:T(1024)S(1)}, u32[]{:S(2)}) copy-start(f32[1280]{0:T(1024)S(1)} %get-tuple-element.3793) | copy-start | bytes 15364
  146.3 4.6 collective-permute-start
  296.2 72.4 %copy-start.127 = (f32[4,16]{1,0:T(4,128)}, f32[4,16]{1,0:T(4,128)S(1)}, u32[]{:S(2)}) copy-start(f32[4,16]{1,0:T(4,128)S(1)} %get-tuple-element.6083) | copy-start | bytes 772
  297.0 133.8 %all-gather.36.cloned.1.call-start = ((), (), s32[]{:S(2)}) async-start(), calls=%async_computation.22 | async-start | bytes 2228224 | tf_op jit(solution)/shard_map/all_gather | solution.py:178
  298.8 221.7 %all-gather.38.cloned.1.call-start = ((), (), s32[]{:S(2)}) async-start(), calls=%async_computation.23 | async-start | bytes 4456448 | tf_op jit(solution)/shard_map/all_gather | solution.py:175
  299.4 239.8 %all-reduce.36.cloned.1.call-start = ((), (), s32[]{:S(2)}) async-start(), calls=%async_computation.8 | async-start | bytes 2097152 | tf_op jit(solution)/shard_map/psum | solution.py:235
  309.7 60.8 %copy-start.187 = (f32[16]{0:T(128)}, f32[16]{0:T(128)S(1)}, u32[]{:S(2)}) copy-start(f32[16]{0:T(128)S(1)} %get-tuple-element.4312) | copy-start | bytes 196
  381.0 53.2 %copy-start.37 = (f32[256,1024]{1,0:T(8,128)}, f32[256,1024]{1,0:T(8,128)S(1)}, u32[]{:S(2)}) copy-start(f32[256,1024]{1,0:T(8,128)S(1)} %reshape.961) | copy-start | bytes 3145732
  383.0 51.2 %copy-start.16 = (f32[256,1024]{1,0:T(8,128)}, f32[256,1024]{1,0:T(8,128)S(1)}, u32[]{:S(2)}) copy-start(f32[256,1024]{1,0:T(8,128)S(1)} %get-tuple-element.4196) | copy-start | bytes 3145732
  385.4 45.4 %copy-start.185 = (f32[256]{0:T(256)}, f32[256]{0:T(256)S(1)}, u32[]{:S(2)}) copy-start(f32[256]{0:T(256)S(1)} %psum.133) | copy-start | bytes 3076
  385.5 48.7 %copy-start.147 = (f32[256]{0:T(256)}, f32[256]{0:T(256)S(1)}, u32[]{:S(2)}) copy-start(f32[256]{0:T(256)S(1)} %add_rsqrt_fusion.1) | copy-start | bytes 3076
  434.2 43.9 %copy-start.96 = (bf16[1,64,256]{2,1,0:T(8,128)(2,1)S(1)}, bf16[1,64,256]{2,1,0:T(8,128)(2,1)}, u32[]{:S(2)}) copy-start(bf16[1,64,256]{2,1,0:T(8,128)(2,1)} %get-tuple-element.4290) | copy-start | bytes 98308
  434.2 286.4 %all-gather.40.cloned.1.call-start = ((), (), s32[]{:S(2)}) async-start(), calls=%async_computation.24 | async-start | bytes 4718592 | tf_op jit(solution)/shard_map/all_gather | solution.py:22
  477.9 70.5 %copy-start.88 = (bf16[1,1024,16]{1,2,0:T(8,128)(2,1)}, bf16[1,1024,16]{1,2,0:T(8,128)(2,1)S(1)}, u32[]{:S(2)}) copy-start(bf16[1,1024,16]{1,2,0:T(8,128)(2,1)S(1)} %copy.403) | copy-start | bytes 98308
  478.0 71.6 %copy-start.115 = (f32[1280]{0:T(1024)}, f32[1280]{0:T(1024)S(1)}, u32[]{:S(2)}) copy-start(f32[1280]{0:T(1024)S(1)} %get-tuple-element.3786) | copy-start | bytes 15364
  478.0 71.6 %copy-start.117 = (f32[1280]{0:T(1024)}, f32[1280]{0:T(1024)S(1)}, u32[]{:S(2)}) copy-start(f32[1280]{0:T(1024)S(1)} %get-tuple-element.3787) | copy-start | bytes 15364
  478.0 71.6 %copy-start.119 = (f32[1280]{0:T(1024)}, f32[1280]{0:T(1024)S(1)}, u32[]{:S(2)}) copy-start(f32[1280]{0:T(1024)S(1)} %get-tuple-element.3789) | copy-start | bytes 15364
  478.1 71.6 %copy-start.121 = (f32[1280]{0:T(1024)}, f32[1280]{0:T(1024)S(1)}, u32[]{:S(2)}) copy-start(f32[1280]{0:T(1024)S(1)} %get-tuple-element.3788) | copy-start | bytes 15364
  544.3 5.1 collective-permute-start.2
  634.9 164.1 %copy-start.73 = (f32[4,64,16]{1,2,0:T(8,128)}, f32[4,64,16]{1,2,0:T(8,128)S(1)}, u32[]{:S(2)}) copy-start(f32[4,64,16]{1,2,0:T(8,128)S(1)} %get-tuple-element.2629) | copy-start | bytes 49156
  645.8 137.2 %all-gather.42.cloned.1.call-start = ((), (), s32[]{:S(2)}) async-start(), calls=%async_computation.25 | async-start | bytes 2228224 | tf_op jit(solution)/shard_map/all_gather | solution.py:178
  646.6 204.8 %all-gather.44.cloned.1.call-start = ((), (), s32[]{:S(2)}) async-start(), calls=%async_computation.26 | async-start | bytes 2359296 | tf_op jit(solution)/shard_map/all_gather | solution.py:36
  720.9 145.0 %copy-start.10 = (f32[16,64,128]{2,1,0:T(8,128)}, f32[16,64,128]{2,1,0:T(8,128)S(1)}, u32[]{:S(2)}) copy-start(f32[16,64,128]{2,1,0:T(8,128)S(1)} %get-tuple-element.2636) | copy-start | bytes 1572868
  733.4 49.7 %copy-start.39 = (f32[256,1024]{1,0:T(8,128)}, f32[256,1024]{1,0:T(8,128)S(1)}, u32[]{:S(2)}) copy-start(f32[256,1024]{1,0:T(8,128)S(1)} %reshape.966) | copy-start | bytes 3145732
  735.4 54.4 %copy-start.12 = (f32[256,1024]{1,0:T(8,128)}, f32[256,1024]{1,0:T(8,128)S(1)}, u32[]{:S(2)}) copy-start(f32[256,1024]{1,0:T(8,128)S(1)} %get-tuple-element.4190) | copy-start | bytes 3145732
  737.8 51.9 %copy-start.102 = (f32[256]{0:T(256)}, f32[256]{0:T(256)S(1)}, u32[]{:S(2)}) copy-start(f32[256]{0:T(256)S(1)} %add_rsqrt_fusion) | copy-start | bytes 3076
  803.3 259.7 %all-reduce.40.cloned.1.call-start = ((), (), s32[]{:S(2)}) async-start(), calls=%async_computation.10 | async-start | bytes 262144 | tf_op jit(solution)/shard_map/psum | solution.py:289
  803.4 48.0 %copy-start.79 = (bf16[4,64,128]{2,1,0:T(8,128)(2,1)}, bf16[4,64,128]{2,1,0:T(8,128)(2,1)S(1)}, u32[]{:S(2)}) copy-start(bf16[4,64,128]{2,1,0:T(8,128)(2,1)S(1)} %fusion.403) | copy-start | bytes 196612
  1046.4 49.7 %all-reduce.42.cloned.1.call-start = ((), (), s32[]{:S(2)}) async-start(), calls=%async_computation.11 | async-start | bytes 1048576 | tf_op jit(solution)/shard_map/psum | solution.py:310
  1066.9 5.7 collective-permute-start.3
  1076.3 43.5 %all-reduce.38.cloned.1.call-start = ((), (), s32[]{:S(2)}) async-start(), calls=%async_computation.9 | async-start | bytes 2097152 | tf_op jit(solution)/shard_map/psum | solution.py:235
  1079.8 112.8 %all-gather.46.cloned.1.call-start = ((), (), s32[]{:S(2)}) async-start(), calls=%async_computation.27 | async-start | bytes 2359296 | tf_op jit(solution)/shard_map/all_gather | solution.py:36
  1142.2 250.9 %all-reduce.44.cloned.1.call-start = ((), (), s32[]{:S(2)}) async-start(), calls=%async_computation.12 | async-start | bytes 262144 | tf_op jit(solution)/shard_map/psum | solution.py:289
  1376.5 52.0 %all-reduce.46.cloned.1.call-start = ((), (), s32[]{:S(2)}) async-start(), calls=%async_computation.13 | async-start | bytes 1048576 | tf_op jit(solution)/shard_map/psum | solution.py:310
  1400.0 5.7 collective-permute-start.4
  1408.6 100.9 %reduce-scatter.27.cloned.1.call-start = ((), (), s32[]{:S(2)}) async-start(), calls=%async_computation.29 | async-start | bytes 557056
  1410.0 175.5 %reduce-scatter.25.cloned.1.call-start = ((), (), s32[]{:S(2)}) async-start(), calls=%async_computation.28 | async-start | bytes 557056
  1412.7 285.8 %all-reduce.48.cloned.1.call-start = ((), (), s32[]{:S(2)}) async-start(), calls=%async_computation.30 | async-start | bytes 141312 | tf_op jit(solution)/shard_map/psum | solution.py:410
  1431.7 347.6 %reduce-scatter.19.cloned.1.call-start = ((), (), s32[]{:S(2)}) async-start(), calls=%async_computation.17 | async-start | bytes 1114112 | tf_op jit(solution)/shard_map/reduce_scatter | solution.py:317
  1434.0 422.7 %reduce-scatter.17.cloned.1.call-start = ((), (), s32[]{:S(2)}) async-start(), calls=%async_computation.16 | async-start | bytes 1114112 | tf_op jit(solution)/shard_map/reduce_scatter | solution.py:317
  1435.5 516.8 %reduce-scatter.23.cloned.1.call-start = ((), (), s32[]{:S(2)}) async-start(), calls=%async_computation.19 | async-start | bytes 4456448 | tf_op jit(solution)/shard_map/reduce_scatter | solution.py:318
  1438.4 611.3 %reduce-scatter.21.cloned.1.call-start = ((), (), s32[]{:S(2)}) async-start(), calls=%async_computation.18 | async-start | bytes 4456448 | tf_op jit(solution)/shard_map/reduce_scatter | solution.py:318
  1442.8 786.3 %reduce-scatter.15.cloned.1.call-start = ((), (), s32[]{:S(2)}) async-start(), calls=%async_computation.15 | async-start | bytes 8912896 | tf_op jit(solution)/shard_map/reduce_scatter | solution.py:315
  1457.2 951.8 %reduce-scatter.13.cloned.1.call-start = ((), (), s32[]{:S(2)}) async-start(), calls=%async_computation.14 | async-start | bytes 8912896 | tf_op jit(solution)/shard_map/reduce_scatter | solution.py:315
  1465.7 121.2 %copy-start.181 = (f32[256]{0:T(256)S(1)}, f32[256]{0:T(256)}, u32[]{:S(2)}) copy-start(f32[256]{0:T(256)} %copy-done.180) | copy-start | bytes 3076
  1465.7 121.2 %copy-start.69 = (f32[256,1024]{1,0:T(8,128)S(1)}, f32[256,1024]{1,0:T(8,128)}, u32[]{:S(2)}) copy-start(f32[256,1024]{1,0:T(8,128)} %get-tuple-element.4326) | copy-start | bytes 3145732
  (248 other events, 1626.9 us)
Sparse Core Ops, SparseCore 0:
  11.4 82.8 all-gather.31
  297.1 71.3 all-gather.33
  371.9 58.9 all-gather.35
  434.0 83.1 all-gather.37
  520.0 19.0 all-reduce.35
  645.9 74.6 all-gather.39
  724.0 58.9 all-gather.41
  803.4 47.9 all-gather.43
  1046.5 16.4 all-reduce.39
  1076.3 19.7 all-reduce.41
  1099.1 20.6 all-reduce.37
  1142.3 50.2 all-gather.45
  1376.6 16.4 all-reduce.43
  1408.7 19.7 all-reduce.45
  1430.6 78.7 reduce-scatter.26
  1511.5 73.9 reduce-scatter.24
  1592.9 105.4 all-reduce.47
  1700.6 78.6 reduce-scatter.18
  1781.5 75.1 reduce-scatter.16
  1858.9 93.3 reduce-scatter.22
  1954.6 95.0 reduce-scatter.20
  2052.0 177.0 reduce-scatter.14
  2231.4 177.5 reduce-scatter.12
where the time goes:
time: 2440 us; the launch traced here: 2420 us
  waiting for transfers between devices  1270 us (52%)
  local copies, waits for them, and re-layouts  329 us (13%)
  blocking collectives  281 us (12%)
  other arithmetic  271 us (11%)
  matrix products  227 us (9%)
    reduce_scatter x2, waiting for transfers between devices, layer_backward(): lax.psum_scatter(grad_in, ('fsdp', 'ctx'), scatter_dimension=0, tiled=True)  357 us
    reduce_scatter x2, waiting for transfers between devices, layer_backward(): lax.psum_scatter(grad_out, ('fsdp', 'ctx'), scatter_dimension=0, tiled=True)  191 us
    reduce_scatter x2, waiting for transfers between devices, layer_backward(): lax.psum_scatter(grad_state, ('fsdp', 'ctx'), scatter_dimension=0, tiled=...  147 us
    unnamed x25, waiting for transfers between devices  120 us
    psum x1, waiting for transfers between devices, on_device(): lax.psum((small_stack[0], kernels_all[:, :, :local_inner], offsets_all[:,...  110 us
    all_gather x2, waiting for transfers between devices, fetch_weights(): lax.all_gather(out_proj[ordinal], ('fsdp', 'ctx'), axis=0, tiled=True)  90.6 us
    all_gather x2, blocking collectives, fetch_weights(): lax.all_gather(step_proj[ordinal], ('fsdp', 'ctx'), axis=0, tiled=True)  86.4 us
    all_gather x2, blocking collectives, fetch_weights(): lax.all_gather(state_proj[ordinal], ('fsdp', 'ctx'), axis=0, tiled=True)  81.5 us
  transfers between devices with their start and end apart: 28, of which 25 were waited for; matrix products, arithmetic and copies ran while one was open for 6% of the time, Pallas kernels for 0%

commit v1 on v0

v1 whole, which is shorter than its diff:
```python
import functools

import jax
import jax.numpy as jnp
from jax import lax
from jax.experimental import pallas as pl
from jax.experimental.pallas import tpu as pltpu
from jax.sharding import PartitionSpec as P

EPSILON = 1e-05
HIGHEST = lax.Precision.HIGHEST
LANES = 128
HALO = 8
ROWS = ("fsdp", "ctx")
HIDE = -1e30
F32 = jnp.float32
BF16 = jnp.bfloat16

INFLOW, CLOSING, AHEAD = 8, 9, 16
BIAS, DECAY, SKIP = 0, 1, 2


def shifted(block, axis, distance):
    devices = range(lax.axis_size(axis))
    route = [(i - distance, i) for i in devices if i - distance in devices]
    return lax.ppermute(block, axis, route)


def swapped(block, axis):
    count = lax.axis_size(axis)
    return lax.ppermute(block, axis, [(i, (i + 1) % count) for i in range(count)])


def pair_sum(block, axis):
    total, moving = (block.astype(F32), block)
    for _ in range(lax.axis_size(axis) - 1):
        moving = swapped(moving, axis)
        total = total + moving.astype(F32)
    return total


def mm(a, b, ca, cb):
    return lax.dot_general(a, b, (((ca,), (cb,)), ((), ())), preferred_element_type=F32)


def fine(a, b, ca, cb):
    return lax.dot_general(
        a, b, (((ca,), (cb,)), ((), ())), precision=HIGHEST, preferred_element_type=F32
    )


def sigmoid(v):
    return 1.0 / (1.0 + jnp.exp(-v))


def lower_ones(length):
    row = lax.broadcasted_iota(jnp.int32, (length, length), 0)
    col = lax.broadcasted_iota(jnp.int32, (length, length), 1)
    return (row >= col).astype(F32)


def spread(table, tile, size):
    per = LANES // size
    lane = lax.broadcasted_iota(jnp.int32, (table.shape[0], LANES), 1)
    first = tile * per
    out = jnp.broadcast_to(table[:, first : first + 1], lane.shape)
    for k in range(1, per):
        column = jnp.broadcast_to(table[:, first + k : first + k + 1], lane.shape)
        out = jnp.where(lane >= k * size, column, out)
    return out


def head_columns(tile, size):
    row = lax.broadcasted_iota(jnp.int32, (LANES, LANES), 0)
    col = lax.broadcasted_iota(jnp.int32, (LANES, LANES), 1)
    return (row // size + tile * (LANES // size) == col).astype(F32)


def tiles_of(width):
    return [(j, slice(j * LANES, (j + 1) * LANES)) for j in range(width // LANES)]


def step_sizes(pre, bias):
    v = pre + bias
    return jnp.maximum(v, 0.0) + jnp.log1p(jnp.exp(-jnp.abs(v)))


def front_kernel(dims, proj, where_, taps, heads, z, act, xs, step, cum, closing):
    tokens, inner, state, lags, size = dims
    for _, cols in tiles_of(inner + 2 * state):
        source = slice(inner + cols.start, inner + cols.stop)
        total = jnp.broadcast_to(taps[lags : lags + 1, cols], (tokens, LANES))
        for k in range(lags):
            begin = HALO - lags + 1 + k
            piece = taps[k : k + 1, cols] * proj[begin : begin + tokens, source]
            if k < lags - 1:
                piece = piece * where_[:, k : k + 1]
            total = total + piece
        z[:, cols] = total
        act[:, cols] = total * sigmoid(total)
    steps = step_sizes(proj[HALO:, 2 * inner + 2 * state :], heads[BIAS : BIAS + 1, :])
    rate = -jnp.exp(heads[DECAY : DECAY + 1, :])
    summed = fine(lower_ones(tokens), steps * rate, 1, 0)
    step[...] = steps
    cum[...] = summed
    ending = jnp.exp(summed[tokens - 1 :, :] - summed) * where_[:, CLOSING : CLOSING + 1]
    write = act[:, inner : inner + state]
    for j, cols in tiles_of(inner):
        scaled = act[:, cols] * spread(steps, j, size)
        xs[:, cols] = scaled
        closing[cols, :] = fine(scaled * spread(ending, j, size), write, 0, 0)


def within_kernel(dims, act, xs, cum, hide, heads, within):
    tokens, inner, state, lags, size = dims
    write, read = (act[:, inner : inner + state], act[:, inner + state :])
    scores = fine(read, write, 1, 1)
    sums = cum[...]
    sums_t = sums.T
    hidden = hide[...]
    lane = lax.broadcasted_iota(jnp.int32, (tokens, LANES), 1)
    per = LANES // size
    for j, cols in tiles_of(inner):
        x = xs[:, cols]
        out = None
        for k in range(per):
            h = j * per + k
            decay = jnp.exp(sums[:, h : h + 1] - sums_t[h : h + 1, :] + hidden)
            y = fine(scores * decay, x, 1, 0)
            out = y if k == 0 else jnp.where(lane >= k * size, y, out)
        within[:, cols] = out + spread(heads[SKIP : SKIP + 1, :], j, size) * act[:, cols]


def join_kernel(dims, within, act, incoming, cum, where_, gate, mixed, gated, squares):
    tokens, inner, state, lags, size = dims
    read = act[:, inner + state :]
    inflow = jnp.exp(cum[...]) * where_[:, INFLOW : INFLOW + 1]
    total = jnp.zeros((tokens, LANES), F32)
    for j, cols in tiles_of(inner):
        reached = fine(read, incoming[cols, :], 1, 1)
        m = within[:, cols] + spread(inflow, j, size) * reached
        g = gate[HALO:, cols]
        v = m * (g * sigmoid(g))
        mixed[:, cols] = m
        gated[:, cols] = v
        total = total + v * v
    squares[...] = fine(jnp.ones((8, LANES), F32), total, 1, 1)


def gate_back_kernel(
    dims, pulled, gated, mixed, gate, factors, gain, act, cum, where_, dy, dgate, carried, dgain
):
    tokens, inner, state, lags, size = dims
    scale, other = (factors[:, 0:1], factors[:, 1:2])
    read = act[:, inner + state :]
    inflow = jnp.exp(cum[...]) * where_[:, INFLOW : INFLOW + 1]
    for j, cols in tiles_of(inner):
        b = pulled[:, cols]
        v = gated[:, cols]
        bs = b * scale
        d = bs * gain[:, cols] - v * other
        dgain[:, cols] = jnp.sum(bs * v, axis=0, keepdims=True)
        g = gate[HALO:, cols]
        s = sigmoid(g)
        dm = d * (g * s)
        dy[:, cols] = dm
        dgate[:, cols] = (d * mixed[:, cols] * (s * (1.0 + g * (1.0 - s)))).astype(BF16)
        carried[cols, :] = fine(spread(inflow, j, size) * dm, read, 0, 0).astype(BF16)


def within_back_kernel(dims, act, xs, cum, hide, dy, dxs, dmaps):
    tokens, inner, state, lags, size = dims
    write, read = (act[:, inner : inner + state], act[:, inner + state :])
    scores = fine(read, write, 1, 1)
    sums = cum[...]
    sums_t = sums.T
    hidden = hide[...]
    lane = lax.broadcasted_iota(jnp.int32, (tokens, LANES), 1)
    per = LANES // size
    dscores = jnp.zeros((tokens, tokens), F32)
    for j, cols in tiles_of(inner):
        x = xs[:, cols]
        d = dy[:, cols]
        out = None
        for k in range(per):
            h = j * per + k
            decay = jnp.exp(sums[:, h : h + 1] - sums_t[h : h + 1, :] + hidden)
            y = fine(scores * decay, d, 0, 0)
            out = y if k == 0 else jnp.where(lane >= k * size, y, out)
            own = jnp.where((lane >= k * size) & (lane < (k + 1) * size), d, 0.0)
            dscores = dscores + fine(own, x, 1, 1) * decay
        dxs[:, cols] = out
    dmaps[:, :state] = fine(dscores, read, 0, 0)
    dmaps[:, state:] = fine(dscores, write, 1, 0)


def finish_kernel(
    dims,
    dxs_within,
    dmaps_within,
    dy,
    xs,
    act,
    z,
    mixed,
    cum,
    step,
    step_pre,
    where_,
    heads,
    adjoint,
    incoming,
    dz,
    dmaps,
    dstep,
    dheads,
):
    tokens, inner, state, lags, size = dims
    write = act[:, inner : inner + state]
    sums, steps = (cum[...], step[...])
    last = sums[tokens - 1 :, :]
    inflow = jnp.exp(sums) * where_[:, INFLOW : INFLOW + 1]
    ending = jnp.exp(last - sums) * where_[:, CLOSING : CLOSING + 1]
    passing = inflow[tokens - 1 :, :]
    dwrite = dmaps_within[:, :state]
    dread = dmaps_within[:, state:]
    dcum = jnp.zeros((tokens, LANES), F32)
    dstep_size = jnp.zeros((tokens, LANES), F32)
    dlast = jnp.zeros((1, LANES), F32)
    dpass = jnp.zeros((1, LANES), F32)
    dskip = jnp.zeros((1, LANES), F32)
    skip = heads[SKIP : SKIP + 1, :]
    for j, cols in tiles_of(inner):
        pick = head_columns(j, size)
        x, v, d = (xs[:, cols], act[:, cols], dy[:, cols])
        later = adjoint[cols, :]
        earlier = incoming[cols, :]
        end = spread(ending, j, size)
        skipped = spread(skip, j, size)
        ends = end * x
        reach = fine(write, later, 1, 1)
        dx = dxs_within[:, cols] + end * reach
        dwrite = dwrite + fine(ends, later, 1, 0)
        dread = dread + fine(spread(inflow, j, size) * d, earlier, 1, 0)
        dvalue = spread(steps, j, size) * dx + skipped * d
        zt = z[:, cols]
        s = sigmoid(zt)
        dz[:, cols] = dvalue * (s * (1.0 + zt * (1.0 - s)))
        dcum = dcum + fine(d * (mixed[:, cols] - skipped * v) - x * dx, pick, 1, 0)
        dstep_size = dstep_size + fine(dx * v, pick, 1, 0)
        dlast = dlast + fine(jnp.sum(ends * reach, axis=0, keepdims=True), pick, 1, 0)
        dskip = dskip + fine(jnp.sum(d * v, axis=0, keepdims=True), pick, 1, 0)
        across = fine(later * earlier, pick, 0, 0)
        dpass = dpass + jnp.sum(across, axis=0, keepdims=True)
    row = lax.broadcasted_iota(jnp.int32, (tokens, LANES), 0)
    dcum = dcum + jnp.where(row == tokens - 1, dlast + passing * dpass, 0.0)
    dlog = fine(lower_ones(tokens), dcum, 0, 0)
    rate = -jnp.exp(heads[DECAY : DECAY + 1, :])
    pre = step_pre[HALO:, :] + heads[BIAS : BIAS + 1, :]
    head = lax.broadcasted_iota(jnp.int32, (tokens, LANES), 1)
    dpre = jnp.where(head < inner // size, (dstep_size + dlog * rate) * sigmoid(pre), 0.0)
    dstep[...] = dpre
    dmaps[:, :state] = dwrite.astype(BF16)
    dmaps[:, state:] = dread.astype(BF16)
    dheads[...] = jnp.zeros(dheads.shape, F32)
    dheads[BIAS : BIAS + 1, :] = jnp.sum(dpre, axis=0, keepdims=True)
    dheads[DECAY : DECAY + 1, :] = jnp.sum(dlog * steps, axis=0, keepdims=True) * rate
    dheads[SKIP : SKIP + 1, :] = dskip


def conv_back_kernel(
    dims, dz, dz_maps, dz_after, dgate, dstep, proj, where_, taps, dpre, dtaps, padded
):
    tokens, inner, state, lags, size = dims
    padded[:tokens, :inner] = dz[...]
    padded[:tokens, inner:] = dz_maps[...]
    padded[tokens:, :] = dz_after[...]
    dpre[:, :inner] = dgate[...]
    dpre[:, 2 * inner + 2 * state :] = dstep[...].astype(BF16)
    dtaps[...] = jnp.zeros(dtaps.shape, F32)
    for _, cols in tiles_of(inner + 2 * state):
        shifted_cols = slice(inner + cols.start, inner + cols.stop)
        d = padded[:tokens, cols]
        total = taps[lags - 1 : lags, cols] * d
        for a in range(1, lags):
            piece = taps[lags - 1 - a : lags - a, cols] * padded[a : a + tokens, cols]
            total = total + piece * where_[:, AHEAD + a : AHEAD + a + 1]
        dpre[:, shifted_cols] = total.astype(BF16)
        for k in range(lags):
            begin = HALO - lags + 1 + k
            piece = d * proj[begin : begin + tokens, shifted_cols]
            if k < lags - 1:
                piece = piece * where_[:, k : k + 1]
            dtaps[k : k + 1, cols] = jnp.sum(piece, axis=0, keepdims=True)
        dtaps[lags : lags + 1, cols] = jnp.sum(d, axis=0, keepdims=True)


def call(kernel, dims, outs, *args, scratch=(), flops=0):
    shapes = [jax.ShapeDtypeStruct(shape, kind) for shape, kind in outs]
    moved = sum(a.size * a.dtype.itemsize for a in args)
    moved += sum(s.size * s.dtype.itemsize for s in shapes)
    return pl.pallas_call(
        functools.partial(kernel, dims),
        out_shape=shapes,
        in_specs=[pl.BlockSpec(memory_space=pltpu.VMEM)] * len(args),
        out_specs=[pl.BlockSpec(memory_space=pltpu.VMEM)] * len(shapes),
        scratch_shapes=scratch,
        compiler_params=pltpu.CompilerParams(vmem_limit_bytes=48 << 20),
        cost_estimate=pl.CostEstimate(flops=flops, bytes_accessed=moved, transcendentals=0),
        name=kernel.__name__,
    )(*args)


def rms_normed(residual, gain):
    scale = lax.rsqrt(jnp.mean(residual * residual, axis=1, keepdims=True) + EPSILON)
    return (residual * scale * gain[None, :]).astype(BF16)


def prefix_factors(decays, place):
    peers = decays.shape[0]
    which = jnp.arange(peers)
    low, mid = (which[:, None], which[None, :])
    inside = (mid > low) & (mid < place)
    before = jnp.prod(jnp.where(inside[:, :, None], decays[None], 1.0), axis=1)
    before = jnp.where((which < place)[:, None], before, 0.0)
    inside = (mid < low) & (mid > place)
    after = jnp.prod(jnp.where(inside[:, :, None], decays[None], 1.0), axis=1)
    after = jnp.where((which > place)[:, None], after, 0.0)
    return (before, after)


def combined(factors, states):
    peers, heads = factors.shape
    split = states.reshape(peers, heads, -1, states.shape[-1]).astype(F32)
    return jnp.sum(factors[:, :, None, None] * split, axis=0).reshape(states.shape[1:])


def layer_forward(residual, place, weights, params, table, hide):
    w_cat, w_out = weights
    gain, taps, heads, gate_gain, dims = params
    tokens, inner, state, lags, size = dims
    head_count = inner // size
    halo = shifted(residual[tokens - HALO :], "ctx", 1)
    extended = jnp.concatenate([halo, residual], axis=0)
    normed_all = rms_normed(extended, gain)
    proj = mm(normed_all, w_cat, 1, 0)
    wide = inner + 2 * state
    z, act, xs, step, cum, closing = call(
        front_kernel,
        dims,
        [
            ((tokens, wide), F32),
            ((tokens, wide), F32),
            ((tokens, inner), F32),
            ((tokens, LANES), F32),
            ((tokens, LANES), F32),
            ((inner, state), F32),
        ],
        proj,
        table,
        taps,
        heads,
    )
    passing = (jnp.exp(cum[tokens - 1]) * table[tokens - 1, INFLOW])[:head_count]
    high = passing.astype(BF16)
    low = (passing - high.astype(F32)).astype(BF16)
    marks = jnp.concatenate([high[:, None], low[:, None]], axis=1)
    marks = jnp.pad(marks, ((0, 0), (0, state - 2)))
    sent = jnp.concatenate([closing.astype(BF16), marks], axis=0)
    everyone = lax.all_gather(sent, "ctx")
    (within,) = call(
        within_kernel, dims, [((tokens, inner), F32)], act, xs, cum, hide, heads, flops=10**9
    )
    marks = everyone[:, inner:, :2].astype(F32)
    before, after = prefix_factors(marks[:, :, 0] + marks[:, :, 1], place)
    incoming = combined(before, everyone[:, :inner])
    mixed, gated, squares = call(
        join_kernel,
        dims,
        [((tokens, inner), F32), ((tokens, inner), F32), ((8, tokens), F32)],
        within,
        act,
        incoming,
        cum,
        table,
        proj,
    )
    width = inner * lax.axis_size("tp")
    scaling = lax.rsqrt(pair_sum(squares[0], "tp") / width + EPSILON)
    branch = (gated * scaling[:, None] * gate_gain[None, :]).astype(BF16)
    updated = residual + pair_sum(mm(branch, w_out, 1, 1), "tp")
    saved = (
        normed_all[HALO:],
        branch,
        gated,
        mixed,
        scaling,
        proj,
        z,
        act,
        xs,
        step,
        cum,
        incoming,
        after,
    )
    return (updated, saved)


def layer_backward(upstream, residual, saved, weights, params, table, hide, mine):
    w_cat, w_out = weights
    gain, taps, heads, gate_gain, dims = params
    tokens, inner, state, lags, size = dims
    normed, branch, gated, mixed, scaling, proj, z, act, xs, step, cum, incoming, after = saved
    width = inner * lax.axis_size("tp")
    wide = inner + 2 * state
    outward = upstream.astype(BF16)
    pulled = mm(outward, w_out, 1, 0)
    inward = pair_sum(jnp.sum(pulled * gate_gain[None, :] * gated, axis=1), "tp")
    grad_out = mm(outward, branch, 0, 0).astype(BF16)
    factors = jnp.stack([scaling, scaling * scaling * scaling * inward / width], axis=1)
    factors = jnp.pad(factors, ((0, 0), (0, LANES - 2)))
    dy, dgate, carried, dgain = call(
        gate_back_kernel,
        dims,
        [
            ((tokens, inner), F32),
            ((tokens, inner), BF16),
            ((inner, state), BF16),
            ((1, inner), F32),
        ],
        pulled,
        gated,
        mixed,
        proj,
        factors,
        gate_gain[None, :],
        act,
        cum,
        table,
    )
    everyone = lax.all_gather(carried, "ctx")
    dxs, dmaps = call(
        within_back_kernel,
        dims,
        [((tokens, inner), F32), ((tokens, 2 * state), F32)],
        act,
        xs,
        cum,
        hide,
        dy,
        flops=2 * 10**9,
    )
    adjoint = combined(after, everyone)
    dz, dmaps, dstep, dheads = call(
        finish_kernel,
        dims,
        [
            ((tokens, inner), F32),
            ((tokens, 2 * state), BF16),
            ((tokens, LANES), F32),
            ((8, LANES), F32),
        ],
        dxs,
        dmaps,
        dy,
        xs,
        act,
        z,
        mixed,
        cum,
        step,
        proj[:, 2 * inner + 2 * state :],
        table,
        heads,
        adjoint,
        incoming,
    )
    z_maps = z[:, inner:]
    s = sigmoid(z_maps)
    dz_maps = pair_sum(dmaps, "tp") * (s * (1.0 + z_maps * (1.0 - s)))
    first = jnp.concatenate([dz[:HALO], dz_maps[:HALO]], axis=1)
    dz_after = shifted(first, "ctx", -1)
    dpre, dtaps = call(
        conv_back_kernel,
        dims,
        [((tokens, w_cat.shape[1]), BF16), ((8, wide), F32)],
        dz,
        dz_maps,
        dz_after,
        dgate,
        dstep,
        proj,
        table,
        taps,
        scratch=[pltpu.VMEM((tokens + HALO, wide), F32)],
    )
    partial = mm(dpre * mine[None, :], w_cat, 1, 1).astype(BF16)
    grad_normed = pair_sum(partial, "tp")
    grad_cat = mm(normed, dpre, 0, 0).astype(BF16)
    shards = (
        lax.psum_scatter(grad_cat, ROWS, scatter_dimension=0, tiled=True),
        lax.psum_scatter(grad_out, ROWS, scatter_dimension=0, tiled=True),
    )
    scale = lax.rsqrt(jnp.mean(residual * residual, axis=1, keepdims=True) + EPSILON)
    grad_gain = jnp.sum(grad_normed * residual * scale, axis=0)
    pull = grad_normed * gain[None, :]
    along = jnp.mean(pull * residual, axis=1, keepdims=True)
    upstream = upstream + pull * scale - residual * (scale * scale * scale * along)
    small = jnp.concatenate(
        [
            grad_gain.reshape(-1, LANES),
            dtaps[: lags + 1].reshape(-1, LANES),
            dheads[:3],
            dgain.reshape(-1, LANES),
        ],
        axis=0,
    )
    return (upstream, shards, small)


def on_device(
    hidden_in,
    segments,
    cotangent,
    norm_gain,
    in_proj,
    step_proj,
    state_proj,
    out_proj,
    conv_inner,
    inner_bias,
    conv_state,
    state_bias,
    step_bias,
    decay_log,
    skip_scale,
    gate_gain,
):
    layer_count, rows, _, inner = in_proj.shape
    tokens = segments.shape[1]
    model = hidden_in.shape[2]
    lags = conv_inner.shape[1]
    state = state_proj.shape[2] // 2
    head_count = step_proj.shape[2]
    size = inner // head_count
    wide = inner + 2 * state
    dims = (tokens, inner, state, lags, size)
    place = lax.axis_index("ctx")

    gathered = []
    for l in range(layer_count):
        steps = jnp.pad(step_proj[l], ((0, 0), (0, LANES - head_count)))
        packed = jnp.concatenate(
            [in_proj[l].reshape(rows, 2 * inner), state_proj[l], steps], axis=1
        )
        w_cat = lax.all_gather(packed, ROWS, axis=0, tiled=True)
        w_out = lax.all_gather(out_proj[l], ROWS, axis=0, tiled=True)
        gathered.append((w_cat, w_out))

    per_shard = norm_gain.shape[0]
    heads_in = jnp.stack([step_bias, decay_log, skip_scale], axis=1)
    heads_in = jnp.pad(heads_in, ((0, 0), (0, 5), (0, LANES - head_count)))
    taps_in = jnp.concatenate(
        [
            jnp.concatenate([conv_inner, conv_state], axis=2),
            jnp.concatenate([inner_bias, state_bias], axis=1)[:, None, :],
        ],
        axis=1,
    )
    flat = jnp.concatenate(
        [
            norm_gain.reshape(per_shard, -1, LANES),
            gate_gain.reshape(per_shard, -1, LANES),
            taps_in.reshape(per_shard, -1, LANES),
            heads_in,
        ],
        axis=1,
    )
    flat = lax.all_gather(flat, "fsdp", axis=0, tiled=True)
    a = model // LANES
    b = a + inner // LANES
    c = b + (lags + 1) * wide // LANES

    labels = segments[0]
    fore = shifted(labels[tokens - HALO :], "ctx", 1)
    aft = shifted(labels[:HALO], "ctx", -1)
    around = jnp.concatenate([fore, labels, aft], axis=0)
    columns = [jnp.zeros((tokens,), F32)] * LANES
    for k in range(lags - 1):
        begin = HALO - lags + 1 + k
        columns[k] = (around[begin : begin + tokens] == labels).astype(F32)
    for k in range(1, lags):
        columns[AHEAD + k] = (around[HALO + k : HALO + k + tokens] == labels).astype(F32)
    columns[INFLOW] = (labels == fore[HALO - 1]).astype(F32)
    columns[CLOSING] = (labels == labels[tokens - 1]).astype(F32)
    table = jnp.stack(columns, axis=1)
    at = jnp.arange(tokens)
    visible = (at[:, None] >= at[None, :]) & (labels[:, None] == labels[None, :])
    hide = jnp.where(visible, 0.0, HIDE).astype(F32)

    pairs = lax.axis_size("tp")
    column = jnp.arange(2 * inner + 2 * state + LANES)
    shared = (column >= 2 * inner) & (column < 2 * inner + 2 * state)
    owner = (column - 2 * inner) * pairs // (2 * state)
    mine = (~shared | (owner == lax.axis_index("tp"))).astype(BF16)

    residual = hidden_in[0].astype(F32)
    residuals, records, layer_params = ([], [], [])
    for l in range(layer_count):
        taps = jnp.pad(flat[l, b:c].reshape(lags + 1, wide), ((0, 7 - lags), (0, 0)))
        params = (flat[l, :a].reshape(-1), taps, flat[l, c:], flat[l, a:b].reshape(-1), dims)
        residuals.append(residual)
        residual, saved = layer_forward(residual, place, gathered[l], params, table, hide)
        records.append(saved)
        layer_params.append(params)
    hidden_out = residual.astype(BF16)[None]

    upstream = cotangent[0].astype(F32)
    cats, outs, smalls = ([None] * layer_count for _ in range(3))
    for l in reversed(range(layer_count)):
        upstream, shards, smalls[l] = layer_backward(
            upstream, residuals[l], records[l], gathered[l], layer_params[l], table, hide, mine
        )
        cats[l], outs[l] = shards

    cat = jnp.stack(cats, axis=0).astype(F32)
    grad_in = cat[:, :, : 2 * inner].reshape(in_proj.shape)
    grad_state = cat[:, :, 2 * inner : 2 * inner + 2 * state]
    grad_step = cat[:, :, 2 * inner + 2 * state : 2 * inner + 2 * state + head_count]
    grad_out = jnp.stack(outs, axis=0).astype(F32)

    small = jnp.stack(smalls, axis=0)
    pieces = lax.all_gather(small, ROWS)
    first_layer = lax.axis_index("fsdp") * per_shard
    small = jnp.sum(lax.dynamic_slice_in_dim(pieces, first_layer, per_shard, 1), axis=0)
    d = a + (lags + 1) * wide // LANES
    taps_out = small[:, a:d].reshape(per_shard, lags + 1, wide)
    heads_out = small[:, d : d + 3, :head_count]
    return (
        hidden_out,
        upstream[None],
        small[:, :a].reshape(per_shard, model),
        grad_in,
        grad_step,
        grad_state,
        grad_out,
        taps_out[:, :lags, :inner],
        taps_out[:, lags, :inner],
        taps_out[:, :lags, inner:],
        taps_out[:, lags, inner:],
        heads_out[:, BIAS],
        heads_out[:, DECAY],
        heads_out[:, SKIP],
        small[:, d + 3 :].reshape(per_shard, inner),
    )


def solution(mesh):
    wide, thin = (P("fsdp", "ctx", None), P("fsdp", "tp"))
    weights = (
        P(None, ROWS, None, "tp"),
        P(None, ROWS, "tp"),
        P(None, ROWS, None),
        P(None, ROWS, "tp"),
    )
    small = (
        P("fsdp", None, "tp"),
        thin,
        P("fsdp", None, None),
        P("fsdp", None),
        thin,
        thin,
        thin,
        thin,
    )
    return jax.shard_map(
        on_device,
        mesh=mesh,
        in_specs=(wide, P("fsdp", "ctx"), wide, P("fsdp", None)) + weights + small,
        out_specs=(wide, wide, P("fsdp", None)) + weights + small,
        check_vma=False,
    )
```

time: 2440 us -> 1060 us (0.43)
  waiting for transfers between devices: 1270 us -> 786 us
  blocking collectives: 281 us -> 4.67 us
  local copies, waits for them, and re-layouts: 329 us -> 64.9 us
  other arithmetic: 271 us -> 39.1 us
  matrix products: 227 us -> 44.6 us
  Pallas kernels: 0 us -> 76.1 us
    reduce_scatter x6 -> x4, waiting for transfers between devices: 696 us -> 340 us  [the longest x2 220 us: layer_backward(): lax.psum_scatter(grad_cat, ROWS, scatter_dimension=0, tiled=True)]
    all_gather x13 -> x1, blocking collectives: 207 us -> 4.67 us  [on_device(): flat = lax.all_gather(flat, 'fsdp', axis=0, tiled=True)]
    psum x7 -> x0, waiting for transfers between devices: 202 us -> none  [the longest x1 110 us: on_device(): lax.psum((small_stack[0], kernels_all[:, :, :local_inner], offsets_all[:,...]
    all_gather x8 -> x9, waiting for transfers between devices: 239 us -> 426 us  [the longest x2 133 us: on_device(): w_cat = lax.all_gather(packed, ROWS, axis=0, tiled=True)]
    dot_general x104 -> x12, matrix products: 224 us -> 44.6 us  [mm(): lax.dot_general(a, b, (((ca,), (cb,)), ((), ())), preferred_element_type=...]
    unnamed x25 -> x13, waiting for transfers between devices: 120 us -> 0.72 us
    pallas_call x0 -> x14, Pallas kernels: none -> 76.1 us  [call(): pl.pallas_call(functools.partial(kernel, dims), out_shape=shapes, in_spec...]
    dynamic_slice x73 -> x0, local copies, waits for them, and re-layouts: 69.1 us -> none  [the longest x64 57.8 us: duality_core(): lax.map(one_block, (part_values, part_write, part_read, part_step, part_l...]
  transfers between devices with their start and end apart: 28 -> 29, of which waited for: 25 -> 24; matrix products, arithmetic and copies ran while one was open for 6% -> 7% of each run, Pallas kernels for 0% -> 4%
where the time goes in v1:
time: 1060 us; the launch traced here: 1050 us
  waiting for transfers between devices  786 us (74%)
  Pallas kernels  76.1 us (7%)
  local copies, waits for them, and re-layouts  64.9 us (6%)
  matrix products  44.6 us (4%)
  other arithmetic  39.1 us (4%)
  starting transfers between devices  20.7 us (2%)
  between operations  16.5 us (2%)
    reduce_scatter x2, waiting for transfers between devices, layer_backward(): lax.psum_scatter(grad_cat, ROWS, scatter_dimension=0, tiled=True)  220 us
    all_gather x2, waiting for transfers between devices, on_device(): w_cat = lax.all_gather(packed, ROWS, axis=0, tiled=True)  133 us
    reduce_scatter x2, waiting for transfers between devices, layer_backward(): lax.psum_scatter(grad_out, ROWS, scatter_dimension=0, tiled=True)  120 us
    all_gather x2, waiting for transfers between devices, on_device(): w_out = lax.all_gather(out_proj[l], ROWS, axis=0, tiled=True)  104 us
    all_gather x2, waiting for transfers between devices, layer_forward(): everyone = lax.all_gather(sent, 'ctx')  81.1 us
    pallas_call x14, Pallas kernels, call(): pl.pallas_call(functools.partial(kernel, dims), out_shape=shapes, in_spec...  76.1 us
    all_gather x2, waiting for transfers between devices, layer_backward(): everyone = lax.all_gather(carried, 'ctx')  53.5 us
    all_gather x1, waiting for transfers between devices, on_device(): pieces = lax.all_gather(small, ROWS)  53.5 us
  transfers between devices with their start and end apart: 29, of which 24 were waited for; matrix products, arithmetic and copies ran while one was open for 7% of the time, Pallas kernels for 4%

profile of v1, /device:TPU:0, one launch (start us, length us, event | category | flops | bytes accessed | tf_op | source)
XLA Modules:
  0.0 1052.8 jit_solution(14612723607845254829)
XLA Ops:
  8.9 2.1 fusion.61
  13.3 5.5 collective-permute-start.1
  19.1 4.8 collective-permute-start
  24.7 4.7 all_gather.45
  36.5 60.3 %all-gather.17.cloned.1.call-done = bf16[1024,2432]{1,0:T(8,128)(2,1)} async-done(((bf16[64,2432]{1,0:T(8,128)(2,1)}), bf16[1024,2432]{1,0:T(8,128)(2,1)}) %all-gather.17.cloned.1.call-update) | async-done | bytes 4980752 | tf_op jit(solution)/shard_map/all_gather | solution.py:557
  96.8 5.4 fusion.67.proj.gate
  102.2 6.2 front_kernel.2
  110.6 1.7 fusion.27
  112.3 1.7 fusion.63
  116.4 4.1 within_kernel.2.within
  121.5 39.1 %all-gather.21.cloned.1.call-done = bf16[8320,128]{1,0:T(8,128)(2,1)} async-done(((bf16[1040,128]{1,0:T(8,128)(2,1)}), bf16[8320,128]{1,0:T(8,128)(2,1)}) %all-gather.21.cloned.1.call-update) | async-done | bytes 2129936 | tf_op jit(solution)/shard_map/all_gather | solution.py:370
  162.4 3.2 multiply_reduce_fusion.1.incoming
  165.7 3.2 join_kernel.2
  171.1 51.8 %all-gather.23.cloned.1.call-done = bf16[1,1024,1024]{2,1,0:T(8,128)(2,1)} async-done(((bf16[1,64,1024]{2,1,0:T(8,128)(2,1)}), bf16[1,1024,1024]{2,1,0:T(8,128)(2,1)}) %all-gather.23.cloned.1.call-update) | async-done | bytes 2097168 | tf_op jit(solution)/shard_map/all_gather | solution.py:558
  222.9 2.4 fusion.8
  225.4 2.6 collective-permute-done.4
  229.0 3.4 collective-permute-start.5
  234.1 72.8 %all-gather.19.cloned.1.call-done = bf16[1024,2432]{1,0:T(8,128)(2,1)} async-done(((bf16[64,2432]{1,0:T(8,128)(2,1)}), bf16[1024,2432]{1,0:T(8,128)(2,1)}) %all-gather.19.cloned.1.call-update) | async-done | bytes 4980752 | tf_op jit(solution)/shard_map/all_gather | solution.py:557
  306.8 5.4 fusion.68.proj.gate
  312.2 6.2 front_kernel.3
  321.1 1.7 fusion.28
  324.0 4.1 within_kernel.3.within
  329.1 42.1 %all-gather.25.cloned.1.call-done = bf16[8320,128]{1,0:T(8,128)(2,1)} async-done(((bf16[1040,128]{1,0:T(8,128)(2,1)}), bf16[8320,128]{1,0:T(8,128)(2,1)}) %all-gather.25.cloned.1.call-update) | async-done | bytes 2129936 | tf_op jit(solution)/shard_map/all_gather | solution.py:370
  373.0 3.2 multiply_reduce_fusion.incoming
  376.3 3.4 join_kernel.3
  380.7 52.7 %all-gather.27.cloned.1.call-done = bf16[1,1024,1024]{2,1,0:T(8,128)(2,1)} async-done(((bf16[1,64,1024]{2,1,0:T(8,128)(2,1)}), bf16[1,1024,1024]{2,1,0:T(8,128)(2,1)}) %all-gather.27.cloned.1.call-update) | async-done | bytes 2097168 | tf_op jit(solution)/shard_map/all_gather | solution.py:558
  433.4 3.5 multiply_reduce_fusion.11
  443.2 4.0 gate_back_kernel.2
  450.6 1.4 broadcast_select_fusion
  452.7 1.5 mul.385
  459.0 7.6 within_back_kernel.2
  468.3 29.5 %all-gather.29.cloned.1.call-done = bf16[8192,128]{1,0:T(8,128)(2,1)} async-done(((bf16[1024,128]{1,0:T(8,128)(2,1)}), bf16[8192,128]{1,0:T(8,128)(2,1)}) %all-gather.29.cloned.1.call-update) | async-done | bytes 2097168 | tf_op jit(solution)/shard_map/all_gather | solution.py:442
  497.8 2.9 fusion.1.adjoint
  502.0 9.8 finish_kernel.2
  516.3 1.7 collective-permute-start.10
  518.0 2.7 fusion.4
  520.9 1.4 collective-permute-done.10.dz_after
  522.3 2.7 conv_back_kernel.2
  525.1 4.4 convolution_convert_fusion.4
  529.7 1.9 collective-permute-done.11
  534.8 1.7 multiply_reduce_fusion.8
  540.3 4.7 gate_back_kernel.3
  546.9 3.2 convert_bitcast_fusion
  550.1 3.8 convolution_convert_fusion.2
  555.9 1.5 mul.412
  562.1 7.6 within_back_kernel.3
  571.5 24.0 %all-gather.31.cloned.1.call-done = bf16[8192,128]{1,0:T(8,128)(2,1)} async-done(((bf16[1024,128]{1,0:T(8,128)(2,1)}), bf16[8192,128]{1,0:T(8,128)(2,1)}) %all-gather.31.cloned.1.call-update) | async-done | bytes 2097168 | tf_op jit(solution)/shard_map/all_gather | solution.py:442
  595.5 2.8 fusion.adjoint
  599.3 9.8 finish_kernel.3
  611.6 1.5 collective-permute-start.14
  613.1 6.0 collective-permute-done.14.dz_after
  619.1 2.7 conv_back_kernel.3
  621.9 4.5 convolution_convert_fusion.3
  629.7 3.8 convolution_convert_fusion
  634.9 3.8 convolution_convert_fusion.1
  638.7 39.2 %reduce-scatter.11.cloned.1.call-done = bf16[64,1024]{1,0:T(8,128)(2,1)} async-done(((bf16[1024,1024]{1,0:T(8,128)(2,1)}), bf16[64,1024]{1,0:T(8,128)(2,1)}) %reduce-scatter.11.cloned.1.call-update) | async-done | bytes 131088 | tf_op jit(solution)/shard_map/reduce_scatter | solution.py:503
  678.0 80.8 %reduce-scatter.9.cloned.1.call-done = bf16[64,1024]{1,0:T(8,128)(2,1)} async-done(((bf16[1024,1024]{1,0:T(8,128)(2,1)}), bf16[64,1024]{1,0:T(8,128)(2,1)}) %reduce-scatter.9.cloned.1.call-update) | async-done | bytes 131088 | tf_op jit(solution)/shard_map/reduce_scatter | solution.py:503
  758.7 1.8 maximum_convert_fusion.1
  760.5 1.3 subtract_bitcast_fusion
  761.9 53.5 %all-gather.33.cloned.1.call-done = f32[32,69,128]{2,1,0:T(8,128)} async-done(((f32[2,69,128]{2,1,0:T(8,128)}), f32[32,69,128]{2,1,0:T(8,128)}) %all-gather.33.cloned.1.call-update) | async-done | bytes 1130512 | tf_op jit(solution)/shard_map/all_gather | solution.py:634
  820.0 108.3 %reduce-scatter.7.cloned.1.call-done = bf16[64,2432]{1,0:T(8,128)(2,1)} async-done(((bf16[1024,2432]{1,0:T(8,128)(2,1)}), bf16[64,2432]{1,0:T(8,128)(2,1)}) %reduce-scatter.7.cloned.1.call-update) | async-done | bytes 311312 | tf_op jit(solution)/shard_map/reduce_scatter | solution.py:502
  928.3 111.8 %reduce-scatter.5.cloned.1.call-done = bf16[64,2432]{1,0:T(8,128)(2,1)} async-done(((bf16[1024,2432]{1,0:T(8,128)(2,1)}), bf16[64,2432]{1,0:T(8,128)(2,1)}) %reduce-scatter.5.cloned.1.call-update) | async-done | bytes 311312 | tf_op jit(solution)/shard_map/reduce_scatter | solution.py:502
  1040.8 1.4 maximum_convert_fusion.2
  1044.2 1.9 reshape.398
  (425 shorter events, 86.1 us)
Async XLA Ops:
  7.2 11.6 %copy-start.79 = (bf16[1,256,1024]{2,1,0:T(8,128)(2,1)S(1)}, bf16[1,256,1024]{2,1,0:T(8,128)(2,1)}, u32[]{:S(2)}) copy-start(bf16[1,256,1024]{2,1,0:T(8,128)(2,1)} %param.16) | copy-start | bytes 1572868
  7.2 89.6 %all-gather.17.cloned.1.call-start = ((), (), s32[]{:S(2)}) async-start(), calls=%async_computation.4 | async-start | bytes 5292032 | tf_op jit(solution)/shard_map/all_gather | solution.py:557
  11.0 13.5 %copy-start.113 = (f32[1,1024]{1,0:T(1,128)S(1)}, f32[1,1024]{1,0:T(1,128)}, u32[]{:S(2)}) copy-start(f32[1,1024]{1,0:T(1,128)} %param.25) | copy-start | bytes 12292
  11.0 13.5 %copy-start.116 = (f32[1,256]{1,0:T(1,128)S(1)}, f32[1,256]{1,0:T(1,128)}, u32[]{:S(2)}) copy-start(f32[1,256]{1,0:T(1,128)} %param.27) | copy-start | bytes 3076
  11.0 13.5 %copy-start.99 = (f32[1,4,1024]{2,1,0:T(4,128)S(1)}, f32[1,4,1024]{2,1,0:T(4,128)}, u32[]{:S(2)}) copy-start(f32[1,4,1024]{2,1,0:T(4,128)} %param.24) | copy-start | bytes 49156
  11.0 13.5 %copy-start.110 = (f32[1,4,256]{2,1,0:T(4,128)S(1)}, f32[1,4,256]{2,1,0:T(4,128)}, u32[]{:S(2)}) copy-start(f32[1,4,256]{2,1,0:T(4,128)} %param.26) | copy-start | bytes 12292
  11.0 13.6 %copy-start.118 = (f32[1,16]{1,0:T(1,128)S(1)}, f32[1,16]{1,0:T(1,128)}, u32[]{:S(2)}) copy-start(f32[1,16]{1,0:T(1,128)} %param.30) | copy-start | bytes 196
  11.0 13.6 %copy-start.119 = (f32[1,16]{1,0:T(1,128)S(1)}, f32[1,16]{1,0:T(1,128)}, u32[]{:S(2)}) copy-start(f32[1,16]{1,0:T(1,128)} %param.29) | copy-start | bytes 196
  11.0 13.6 %copy-start.120 = (f32[1,16]{1,0:T(1,128)S(1)}, f32[1,16]{1,0:T(1,128)}, u32[]{:S(2)}) copy-start(f32[1,16]{1,0:T(1,128)} %param.28) | copy-start | bytes 196
  11.0 13.6 %copy-start.111 = (f32[1,1024]{1,0:T(1,128)S(1)}, f32[1,1024]{1,0:T(1,128)}, u32[]{:S(2)}) copy-start(f32[1,1024]{1,0:T(1,128)} %param.31) | copy-start | bytes 12292
  11.0 13.6 %copy-start.112 = (f32[1,1024]{1,0:T(1,128)S(1)}, f32[1,1024]{1,0:T(1,128)}, u32[]{:S(2)}) copy-start(f32[1,1024]{1,0:T(1,128)} %param.19) | copy-start | bytes 12292
  11.9 148.7 %all-gather.21.cloned.1.call-start = ((), (), s32[]{:S(2)}) async-start(), calls=%async_computation.10 | async-start | bytes 2396160 | tf_op jit(solution)/shard_map/all_gather | solution.py:370
  12.0 18.6 %collective-permute-start.2 = (s32[8]{0:T(128)S(1)}, s32[8]{0:T(128)S(1)}, u32[]{:S(2)}, u32[]{:S(2)}) collective-permute-start(s32[8]{0:T(128)S(1)} %get-tuple-element.211), channel_id=1, source_target_pairs={{2,0},{4,2},{6,4},{8,6},{10,8},{12,10},{14,12},{3,1},{5,3},{7,5},{... | collective-permute-start | bytes 104 | tf_op jit(solution)/shard_map/ppermute | solution.py:26
  13.3 16.7 %collective-permute-start.1 = (s32[8]{0:T(128)S(1)}, s32[8]{0:T(128)S(1)}, u32[]{:S(2)}, u32[]{:S(2)}) collective-permute-start(s32[8]{0:T(128)S(1)} %get-tuple-element.212), channel_id=1, source_target_pairs={{0,2},{2,4},{4,6},{6,8},{8,10},{10,12},{12,14},{1,3},{3,5},{5,7},{... | collective-permute-start | bytes 104 | tf_op jit(solution)/shard_map/ppermute | solution.py:26
  19.1 17.0 %collective-permute-start = (f32[8,1024]{1,0:T(8,128)S(1)}, f32[8,1024]{1,0:T(8,128)S(1)}, u32[]{:S(2)}, u32[]{:S(2)}) collective-permute-start(f32[8,1024]{1,0:T(8,128)S(1)} %slice_bitcast_fusion), channel_id=1, source_target_pairs={{0,2},{2,4},{4,6},{6,8},{8,10},{10,12},{12,14},{1,3},{3,5},{5,7},{... | collective-permute-start | bytes 98312 | tf_op jit(solution)/shard_map/ppermute | solution.py:26
  30.0 192.9 %copy-start.91 = (f32[1024]{0:T(1024)}, f32[1024]{0:T(1024)S(1)}, u32[]{:S(2)}) copy-start(f32[1024]{0:T(1024)S(1)} %get-tuple-element.181) | copy-start | bytes 12292
  36.4 65.8 %copy-start.84 = (bf16[264,1024]{1,0:T(8,128)(2,1)}, bf16[264,1024]{1,0:T(8,128)(2,1)S(1)}, u32[]{:S(2)}) copy-start(bf16[264,1024]{1,0:T(8,128)(2,1)S(1)} %multiply_convert_fusion.1) | copy-start | bytes 1622020
  109.6 10.9 %copy-start.13 = (f32[256,1024]{1,0:T(8,128)}, f32[256,1024]{1,0:T(8,128)S(1)}, u32[]{:S(2)}) copy-start(f32[256,1024]{1,0:T(8,128)S(1)} %get-tuple-element.58.xs) | copy-start | bytes 3145732
  109.6 10.9 %copy-start.66 = (f32[256,128]{1,0:T(8,128)}, f32[256,128]{1,0:T(8,128)S(1)}, u32[]{:S(2)}) copy-start(f32[256,128]{1,0:T(8,128)S(1)} %get-tuple-element.86.step) | copy-start | bytes 393220
  109.6 56.1 %copy-start.2 = (f32[256,1280]{1,0:T(8,128)}, f32[256,1280]{1,0:T(8,128)S(1)}, u32[]{:S(2)}) copy-start(f32[256,1280]{1,0:T(8,128)S(1)} %get-tuple-element.57.act) | copy-start | bytes 3932164
  109.6 56.1 %copy-start.27 = (f32[256,128]{1,0:T(8,128)}, f32[256,128]{1,0:T(8,128)S(1)}, u32[]{:S(2)}) copy-start(f32[256,128]{1,0:T(8,128)S(1)} %get-tuple-element.59.cum) | copy-start | bytes 393220
  112.3 110.6 %all-gather.23.cloned.1.call-start = ((), (), s32[]{:S(2)}) async-start(), calls=%async_computation.11 | async-start | bytes 2228224 | tf_op jit(solution)/shard_map/all_gather | solution.py:558
  114.0 192.8 %all-gather.19.cloned.1.call-start = ((), (), s32[]{:S(2)}) async-start(), calls=%async_computation.5 | async-start | bytes 5292032 | tf_op jit(solution)/shard_map/all_gather | solution.py:557
  116.0 255.2 %all-gather.25.cloned.1.call-start = ((), (), s32[]{:S(2)}) async-start(), calls=%async_computation.12 | async-start | bytes 2396160 | tf_op jit(solution)/shard_map/all_gather | solution.py:370
  116.2 45.1 %copy-start.117 = (pred[8]{0:T(512)(128)(4,1)}, pred[8]{0:T(512)(128)(4,1)S(1)}, u32[]{:S(2)}) copy-start(pred[8]{0:T(512)(128)(4,1)S(1)} %get-tuple-element.221) | copy-start | bytes 28
  116.3 45.9 %copy-start.114 = (pred[8]{0:T(512)(128)(4,1)}, pred[8]{0:T(512)(128)(4,1)S(1)}, u32[]{:S(2)}) copy-start(pred[8]{0:T(512)(128)(4,1)S(1)} %get-tuple-element.222) | copy-start | bytes 28
  116.3 45.2 %copy-start.106 = (pred[8,8]{1,0:T(8,128)(4,1)}, pred[8,8]{1,0:T(8,128)(4,1)S(1)}, u32[]{:S(2)}) copy-start(pred[8,8]{1,0:T(8,128)(4,1)S(1)} %fusion.44) | copy-start | bytes 196
  116.3 45.2 %copy-start.108 = (pred[8,8]{1,0:T(8,128)(4,1)}, pred[8,8]{1,0:T(8,128)(4,1)S(1)}, u32[]{:S(2)}) copy-start(pred[8,8]{1,0:T(8,128)(4,1)S(1)} %fusion.43) | copy-start | bytes 196
  169.9 55.4 %copy-start.6 = (f32[256,1024]{1,0:T(8,128)}, f32[256,1024]{1,0:T(8,128)S(1)}, u32[]{:S(2)}) copy-start(f32[256,1024]{1,0:T(8,128)S(1)} %get-tuple-element.61.gated) | copy-start | bytes 3145732
  170.0 1.2 collective-permute-start.3
  171.1 54.2 %copy-start.95 = (f32[256]{0:T(256)}, f32[256]{0:T(256)S(1)}, u32[]{:S(2)}) copy-start(f32[256]{0:T(256)S(1)} %add_rsqrt_fusion.5) | copy-start | bytes 3076
  225.4 2.7 collective-permute-start.4
  229.0 83.3 %copy-start.75 = (f32[256,1024]{1,0:T(8,128)}, f32[256,1024]{1,0:T(8,128)S(1)}, u32[]{:S(2)}) copy-start(f32[256,1024]{1,0:T(8,128)S(1)} %get-tuple-element.168) | copy-start | bytes 3145732
  229.0 4.7 collective-permute-start.5
  232.4 79.8 %copy-start.59 = (f32[8,1280]{1,0:T(8,128)}, f32[8,1280]{1,0:T(8,128)S(1)}, u32[]{:S(2)}) copy-start(f32[8,1280]{1,0:T(8,128)S(1)} %pad.37.taps) | copy-start | bytes 122884
  234.1 78.2 %copy-start.86 = (bf16[264,1024]{1,0:T(8,128)(2,1)}, bf16[264,1024]{1,0:T(8,128)(2,1)S(1)}, u32[]{:S(2)}) copy-start(bf16[264,1024]{1,0:T(8,128)(2,1)S(1)} %multiply_convert_fusion) | copy-start | bytes 1622020
  320.2 56.0 %copy-start.4 = (f32[256,1280]{1,0:T(8,128)}, f32[256,1280]{1,0:T(8,128)S(1)}, u32[]{:S(2)}) copy-start(f32[256,1280]{1,0:T(8,128)S(1)} %get-tuple-element.63.act) | copy-start | bytes 3932164
  320.2 56.0 %copy-start.31 = (f32[256,128]{1,0:T(8,128)}, f32[256,128]{1,0:T(8,128)S(1)}, u32[]{:S(2)}) copy-start(f32[256,128]{1,0:T(8,128)S(1)} %get-tuple-element.65.cum) | copy-start | bytes 393220
  322.8 49.2 %copy-start.107 = (pred[8,8]{1,0:T(8,128)(4,1)S(1)}, pred[8,8]{1,0:T(8,128)(4,1)}, u32[]{:S(2)}) copy-start(pred[8,8]{1,0:T(8,128)(4,1)} %copy-done.106) | copy-start | bytes 196
  322.9 49.2 %copy-start.109 = (pred[8,8]{1,0:T(8,128)(4,1)S(1)}, pred[8,8]{1,0:T(8,128)(4,1)}, u32[]{:S(2)}) copy-start(pred[8,8]{1,0:T(8,128)(4,1)} %copy-done.108) | copy-start | bytes 196
  322.9 49.9 %copy-start.115 = (pred[8]{0:T(512)(128)(4,1)S(1)}, pred[8]{0:T(512)(128)(4,1)}, u32[]{:S(2)}) copy-start(pred[8]{0:T(512)(128)(4,1)} %copy-done.114) | copy-start | bytes 28
  322.9 110.6 %all-gather.27.cloned.1.call-start = ((), (), s32[]{:S(2)}) async-start(), calls=%async_computation.13 | async-start | bytes 2228224 | tf_op jit(solution)/shard_map/all_gather | solution.py:558
  323.5 174.3 %all-gather.29.cloned.1.call-start = ((), (), s32[]{:S(2)}) async-start(), calls=%async_computation.14 | async-start | bytes 2359296 | tf_op jit(solution)/shard_map/all_gather | solution.py:442
  380.7 56.2 %copy-start.8 = (f32[256,1024]{1,0:T(8,128)}, f32[256,1024]{1,0:T(8,128)S(1)}, u32[]{:S(2)}) copy-start(f32[256,1024]{1,0:T(8,128)S(1)} %get-tuple-element.67.gated) | copy-start | bytes 3145732
  380.7 56.2 %collective-permute-start.6 = (f32[256]{0:T(256)S(1)}, f32[256]{0:T(256)S(1)}, u32[]{:S(2)}, u32[]{:S(2)}) collective-permute-start(f32[256]{0:T(256)S(1)} %bitcast.227), channel_id=1, source_target_pairs={{0,1},{1,0},{2,3},{3,2},{4,5},{5,4},{6,7},{7,6},{8,9},{9,8},{10,11... | collective-permute-start | bytes 3080 | tf_op jit(solution)/shard_map/ppermute | solution.py:31
  436.9 1.2 collective-permute-start.8
  449.8 145.8 %all-gather.31.cloned.1.call-start = ((), (), s32[]{:S(2)}) async-start(), calls=%async_computation.15 | async-start | bytes 2359296 | tf_op jit(solution)/shard_map/all_gather | solution.py:442
  513.4 1.7 collective-permute-start.9
  513.4 11.7 %copy-start.104 = (bf16[2432]{0:T(1024)(128)(2,1)}, bf16[2432]{0:T(1024)(128)(2,1)S(1)}, u32[]{:S(2)}) copy-start(bf16[2432]{0:T(1024)(128)(2,1)S(1)} %fusion.38) | copy-start | bytes 14596
  516.3 6.0 collective-permute-start.10
  520.7 12.0 %collective-permute-start.7 = (f32[256,1024]{1,0:T(8,128)S(1)}, f32[256,1024]{1,0:T(8,128)S(1)}, u32[]{:S(2)}, u32[]{:S(2)}) collective-permute-start(f32[256,1024]{1,0:T(8,128)S(1)} %fusion.4), channel_id=1, source_target_pairs={{0,1},{1,0},{2,3},{3,2},{4,5},{5,4},{6,7},{7,6},{8,9},{9,8},{10,11... | collective-permute-start | bytes 3145736 | tf_op jit(solution)/shard_map/ppermute | solution.py:31
  529.6 2.0 collective-permute-start.11
  536.5 1.2 collective-permute-start.12
  546.8 131.2 %reduce-scatter.11.cloned.1.call-start = ((), (), s32[]{:S(2)}) async-start(), calls=%async_computation.9 | async-start | bytes 2228224 | tf_op jit(solution)/shard_map/reduce_scatter | solution.py:503
  550.0 208.7 %reduce-scatter.9.cloned.1.call-start = ((), (), s32[]{:S(2)}) async-start(), calls=%async_computation.8 | async-start | bytes 2228224 | tf_op jit(solution)/shard_map/reduce_scatter | solution.py:503
  554.0 261.4 %all-gather.33.cloned.1.call-start = ((), (), s32[]{:S(2)}) async-start(), calls=%async_computation.16 | async-start | bytes 1253376 | tf_op jit(solution)/shard_map/all_gather | solution.py:634
  571.5 26.9 %copy-start.30 = (f32[256,128]{1,0:T(8,128)S(1)}, f32[256,128]{1,0:T(8,128)}, u32[]{:S(2)}) copy-start(f32[256,128]{1,0:T(8,128)} %copy-done.27) | copy-start | bytes 393220
  599.3 19.8 %copy-start.56 = (bf16[256,1024]{1,0:T(8,128)(2,1)S(1)}, bf16[256,1024]{1,0:T(8,128)(2,1)}, u32[]{:S(2)}) copy-start(bf16[256,1024]{1,0:T(8,128)(2,1)} %copy-done.55) | copy-start | bytes 1572868
  609.1 1.4 collective-permute-start.13
  611.6 7.5 collective-permute-start.14
  626.4 2.0 collective-permute-start.15
  629.6 298.7 %reduce-scatter.7.cloned.1.call-start = ((), (), s32[]{:S(2)}) async-start(), calls=%async_computation.7 | async-start | bytes 5292032 | tf_op jit(solution)/shard_map/reduce_scatter | solution.py:502
  633.5 406.6 %reduce-scatter.5.cloned.1.call-start = ((), (), s32[]{:S(2)}) async-start(), calls=%async_computation.6 | async-start | bytes 5292032 | tf_op jit(solution)/shard_map/reduce_scatter | solution.py:502
  638.7 121.8 %copy-start.78 = (f32[256,1024]{1,0:T(8,128)S(1)}, f32[256,1024]{1,0:T(8,128)}, u32[]{:S(2)}) copy-start(f32[256,1024]{1,0:T(8,128)} %copy-done.77) | copy-start | bytes 3145732
  (86 other events, 244.0 us)
Sparse Core Ops, SparseCore 0:
  12.0 84.7 all-gather.16
  112.4 48.1 all-gather.20
  164.0 58.8 all-gather.22
  226.0 80.7 all-gather.18
  323.0 48.1 all-gather.24
  374.4 59.0 all-gather.26
  449.9 47.8 all-gather.28
  546.9 48.5 all-gather.30
  597.8 80.1 reduce-scatter.10
  680.1 78.6 reduce-scatter.8
  762.1 53.2 all-gather.32
  817.6 110.7 reduce-scatter.6
  930.7 109.3 reduce-scatter.4

commit v2 on v1

--- a/solution.py
+++ b/solution.py
@@ -37,6 +37,68 @@
         moving = swapped(moving, axis)
         total = total + moving.astype(F32)
     return total
+
+
+def bits(axis):
+    count = lax.axis_size(axis)
+    assert count & (count - 1) == 0
+    return [(axis, 1 << k) for k in range(count.bit_length() - 1)]
+
+
+def partner(block, axis, bit):
+    return lax.ppermute(block, axis, [(i, i ^ bit) for i in range(lax.axis_size(axis))])
+
+
+def side(axis, bit):
+    return (lax.axis_index(axis) // bit) % 2
+
+
+def shard_bits():
+    return bits("fsdp")[::-1] + bits("ctx")[::-1]
+
+
+def halved_scatter(block, order):
+    left = shard_bits()
+    block = block.reshape((2,) * len(left) + (-1, block.shape[1]))
+    for axis, bit in order:
+        dim = left.index((axis, bit))
+        mine = side(axis, bit)
+        away = lax.dynamic_index_in_dim(block, 1 - mine, dim, False)
+        kept = lax.dynamic_index_in_dim(block, mine, dim, False)
+        left.remove((axis, bit))
+        block = kept.astype(F32) + partner(away, axis, bit).astype(F32)
+        block = block.astype(BF16) if left else block
+    return block
+
+
+def doubled_gather(block, order):
+    every = shard_bits()
+    have = []
+    for axis, bit in order:
+        other = partner(block, axis, bit)
+        have = [b for b in every if b in have or b == (axis, bit)]
+        dim = have.index((axis, bit))
+        low = side(axis, bit) == 0
+        first = jnp.where(low, block, other)
+        second = jnp.where(low, other, block)
+        block = jnp.stack([first, second], axis=dim)
+    return block.reshape(-1, block.shape[-1])
+
+
+def exchanged_sum(block):
+    for axis, bit in shard_bits():
+        block = block + partner(block, axis, bit)
+    return block
+
+
+def scattered(block):
+    (ys, cs) = (bits("fsdp"), bits("ctx"))
+    first = ys + cs
+    second = cs[:1] + ys + cs[1:]
+    cut = block.shape[1] // (2 * LANES) * LANES
+    return jnp.concatenate(
+        [halved_scatter(block[:, :cut], first), halved_scatter(block[:, cut:], second)], axis=1
+    )
 
 
 def mm(a, b, ca, cb):
@@ -83,6 +145,39 @@
 def step_sizes(pre, bias):
     v = pre + bias
     return jnp.maximum(v, 0.0) + jnp.log1p(jnp.exp(-jnp.abs(v)))
+
+
+def put_decay(packed, inner, decay):
+    high = decay.astype(BF16).astype(F32)
+    row = lax.broadcasted_iota(jnp.int32, (16, LANES), 0)
+    packed[inner:, :] = jnp.where(row < 8, high, decay - high).astype(BF16)
+
+
+def get_decay(packed, inner):
+    both = packed[inner:, :].astype(F32)
+    return both[0:1, :] + both[8:9, :]
+
+
+def head_rows(decay, tile, size):
+    return jnp.sum(head_columns(tile, size) * decay, axis=1, keepdims=True)
+
+
+def chained(parts, inner, size, j, cols):
+    total, factor = (parts[0][cols, :].astype(F32), get_decay(parts[0], inner))
+    for part in parts[1:]:
+        total = total + head_rows(factor, j, size) * part[cols, :].astype(F32)
+        factor = factor * get_decay(part, inner)
+    return (total, factor)
+
+
+def fold_kernel(dims, *refs):
+    inner, size = (dims[1], dims[4])
+    parts, packed = (refs[:-1], refs[-1])
+    factor = None
+    for j, cols in tiles_of(inner):
+        total, factor = chained(parts, inner, size, j, cols)
+        packed[cols, :] = total.astype(BF16)
+    put_decay(packed, inner, factor)
 
 
 def front_kernel(dims, proj, where_, taps, heads, z, act, xs, step, cum, closing):
@@ -108,7 +203,9 @@
     for j, cols in tiles_of(inner):
         scaled = act[:, cols] * spread(steps, j, size)
         xs[:, cols] = scaled
-        closing[cols, :] = fine(scaled * spread(ending, j, size), write, 0, 0)
+        closing[cols, :] = fine(scaled * spread(ending, j, size), write, 0, 0).astype(BF16)
+    entering = where_[tokens - 1 :, INFLOW : INFLOW + 1]
+    put_decay(closing, inner, jnp.exp(summed[tokens - 1 :, :]) * entering)
 
 
 def within_kernel(dims, act, xs, cum, hide, heads, within):
@@ -131,13 +228,16 @@
         within[:, cols] = out + spread(heads[SKIP : SKIP + 1, :], j, size) * act[:, cols]
 
 
-def join_kernel(dims, within, act, incoming, cum, where_, gate, mixed, gated, squares):
-    tokens, inner, state, lags, size = dims
+def join_kernel(dims, within, act, cum, where_, gate, *refs):
+    tokens, inner, state, lags, size = dims
+    parts, (mixed, gated, squares, incoming) = (refs[:-4], refs[-4:])
     read = act[:, inner + state :]
     inflow = jnp.exp(cum[...]) * where_[:, INFLOW : INFLOW + 1]
     total = jnp.zeros((tokens, LANES), F32)
     for j, cols in tiles_of(inner):
-        reached = fine(read, incoming[cols, :], 1, 1)
+        entered, _ = chained(parts, inner, size, j, cols)
+        incoming[cols, :] = entered
+        reached = fine(read, entered, 1, 1)
         m = within[:, cols] + spread(inflow, j, size) * reached
         g = gate[HALO:, cols]
         v = m * (g * sigmoid(g))
@@ -166,6 +266,7 @@
         dy[:, cols] = dm
         dgate[:, cols] = (d * mixed[:, cols] * (s * (1.0 + g * (1.0 - s)))).astype(BF16)
         carried[cols, :] = fine(spread(inflow, j, size) * dm, read, 0, 0).astype(BF16)
+    put_decay(carried, inner, inflow[tokens - 1 :, :])
 
 
 def within_back_kernel(dims, act, xs, cum, hide, dy, dxs, dmaps):
@@ -208,14 +309,11 @@
     step_pre,
     where_,
     heads,
-    adjoint,
     incoming,
-    dz,
-    dmaps,
-    dstep,
-    dheads,
+    *refs,
 ):
     tokens, inner, state, lags, size = dims
+    parts, (dz, dmaps, dstep, dheads) = (refs[:-4], refs[-4:])
     write = act[:, inner : inner + state]
     sums, steps = (cum[...], step[...])
     last = sums[tokens - 1 :, :]
@@ -233,7 +331,7 @@
     for j, cols in tiles_of(inner):
         pick = head_columns(j, size)
         x, v, d = (xs[:, cols], act[:, cols], dy[:, cols])
-        later = adjoint[cols, :]
+        later, _ = chained(parts, inner, size, j, cols)
         earlier = incoming[cols, :]
         end = spread(ending, j, size)
         skipped = spread(skip, j, size)
@@ -269,14 +367,13 @@
 
 
 def conv_back_kernel(
-    dims, dz, dz_maps, dz_after, dgate, dstep, proj, where_, taps, dpre, dtaps, padded
+    dims, dz, dz_maps, dz_after, dstep, proj, where_, taps, dpre, dtaps, padded
 ):
     tokens, inner, state, lags, size = dims
     padded[:tokens, :inner] = dz[...]
     padded[:tokens, inner:] = dz_maps[...]
     padded[tokens:, :] = dz_after[...]
-    dpre[:, :inner] = dgate[...]
-    dpre[:, 2 * inner + 2 * state :] = dstep[...].astype(BF16)
+    dpre[:, inner + 2 * state :] = dstep[...].astype(BF16)
     dtaps[...] = jnp.zeros(dtaps.shape, F32)
     for _, cols in tiles_of(inner + 2 * state):
         shifted_cols = slice(inner + cols.start, inner + cols.stop)
@@ -285,7 +382,7 @@
         for a in range(1, lags):
             piece = taps[lags - 1 - a : lags - a, cols] * padded[a : a + tokens, cols]
             total = total + piece * where_[:, AHEAD + a : AHEAD + a + 1]
-        dpre[:, shifted_cols] = total.astype(BF16)
+        dpre[:, cols] = total.astype(BF16)
         for k in range(lags):
             begin = HALO - lags + 1 + k
             piece = d * proj[begin : begin + tokens, shifted_cols]
@@ -316,26 +413,18 @@
     return (residual * scale * gain[None, :]).astype(BF16)
 
 
-def prefix_factors(decays, place):
-    peers = decays.shape[0]
-    which = jnp.arange(peers)
-    low, mid = (which[:, None], which[None, :])
-    inside = (mid > low) & (mid < place)
-    before = jnp.prod(jnp.where(inside[:, :, None], decays[None], 1.0), axis=1)
-    before = jnp.where((which < place)[:, None], before, 0.0)
-    inside = (mid < low) & (mid > place)
-    after = jnp.prod(jnp.where(inside[:, :, None], decays[None], 1.0), axis=1)
-    after = jnp.where((which > place)[:, None], after, 0.0)
-    return (before, after)
-
-
-def combined(factors, states):
-    peers, heads = factors.shape
-    split = states.reshape(peers, heads, -1, states.shape[-1]).astype(F32)
-    return jnp.sum(factors[:, :, None, None] * split, axis=0).reshape(states.shape[1:])
-
-
-def layer_forward(residual, place, weights, params, table, hide):
+def carried_over(packed, direction, dims):
+    reach = max(lax.axis_size("ctx") // 2, 1)
+    far = shifted(packed, "ctx", direction * reach)
+    parts, sending = ([], packed)
+    while len(parts) < reach.bit_length() - 1:
+        parts.append(shifted(sending, "ctx", direction << len(parts)))
+        if len(parts) < reach.bit_length() - 1:
+            (sending,) = call(fold_kernel, dims, [(packed.shape, BF16)], packed, *parts)
+    return parts + [far]
+
+
+def layer_forward(residual, weights, params, table, hide):
     w_cat, w_out = weights
     gain, taps, heads, gate_gain, dims = params
     tokens, inner, state, lags, size = dims
@@ -354,36 +443,32 @@
             ((tokens, inner), F32),
             ((tokens, LANES), F32),
             ((tokens, LANES), F32),
-            ((inner, state), F32),
+            ((inner + 16, state), BF16),
         ],
         proj,
         table,
         taps,
         heads,
     )
-    passing = (jnp.exp(cum[tokens - 1]) * table[tokens - 1, INFLOW])[:head_count]
-    high = passing.astype(BF16)
-    low = (passing - high.astype(F32)).astype(BF16)
-    marks = jnp.concatenate([high[:, None], low[:, None]], axis=1)
-    marks = jnp.pad(marks, ((0, 0), (0, state - 2)))
-    sent = jnp.concatenate([closing.astype(BF16), marks], axis=0)
-    everyone = lax.all_gather(sent, "ctx")
+    parts = carried_over(closing, 1, dims)
     (within,) = call(
         within_kernel, dims, [((tokens, inner), F32)], act, xs, cum, hide, heads, flops=10**9
     )
-    marks = everyone[:, inner:, :2].astype(F32)
-    before, after = prefix_factors(marks[:, :, 0] + marks[:, :, 1], place)
-    incoming = combined(before, everyone[:, :inner])
-    mixed, gated, squares = call(
+    mixed, gated, squares, incoming = call(
         join_kernel,
         dims,
-        [((tokens, inner), F32), ((tokens, inner), F32), ((8, tokens), F32)],
+        [
+            ((tokens, inner), F32),
+            ((tokens, inner), F32),
+            ((8, tokens), F32),
+            ((inner, state), F32),
+        ],
         within,
         act,
-        incoming,
         cum,
         table,
         proj,
+        *parts,
     )
     width = inner * lax.axis_size("tp")
     scaling = lax.rsqrt(pair_sum(squares[0], "tp") / width + EPSILON)
@@ -402,16 +487,15 @@
         step,
         cum,
         incoming,
-        after,
     )
     return (updated, saved)
 
 
-def layer_backward(upstream, residual, saved, weights, params, table, hide, mine):
+def layer_backward(upstream, residual, saved, weights, params, table, hide, mine, last):
     w_cat, w_out = weights
     gain, taps, heads, gate_gain, dims = params
     tokens, inner, state, lags, size = dims
-    normed, branch, gated, mixed, scaling, proj, z, act, xs, step, cum, incoming, after = saved
+    normed, branch, gated, mixed, scaling, proj, z, act, xs, step, cum, incoming = saved
     width = inner * lax.axis_size("tp")
     wide = inner + 2 * state
     outward = upstream.astype(BF16)
@@ -426,7 +510,7 @@
         [
             ((tokens, inner), F32),
             ((tokens, inner), BF16),
-            ((inner, state), BF16),
+            ((inner + 16, state), BF16),
             ((1, inner), F32),
         ],
         pulled,
@@ -439,7 +523,7 @@
         cum,
         table,
     )
-    everyone = lax.all_gather(carried, "ctx")
+    parts = carried_over(carried, -1, dims)
     dxs, dmaps = call(
         within_back_kernel,
         dims,
@@ -451,7 +535,6 @@
         dy,
         flops=2 * 10**9,
     )
-    adjoint = combined(after, everyone)
     dz, dmaps, dstep, dheads = call(
         finish_kernel,
         dims,
@@ -473,8 +556,8 @@
         proj[:, 2 * inner + 2 * state :],
         table,
         heads,
-        adjoint,
         incoming,
+        *parts,
     )
     z_maps = z[:, inner:]
     s = sigmoid(z_maps)
@@ -484,24 +567,28 @@
     dpre, dtaps = call(
         conv_back_kernel,
         dims,
-        [((tokens, w_cat.shape[1]), BF16), ((8, wide), F32)],
+        [((tokens, wide + LANES), BF16), ((8, wide), F32)],
         dz,
         dz_maps,
         dz_after,
-        dgate,
         dstep,
         proj,
         table,
         taps,
         scratch=[pltpu.VMEM((tokens + HALO, wide), F32)],
     )
-    partial = mm(dpre * mine[None, :], w_cat, 1, 1).astype(BF16)
-    grad_normed = pair_sum(partial, "tp")
-    grad_cat = mm(normed, dpre, 0, 0).astype(BF16)
-    shards = (
-        lax.psum_scatter(grad_cat, ROWS, scatter_dimension=0, tiled=True),
-        lax.psum_scatter(grad_out, ROWS, scatter_dimension=0, tiled=True),
-    )
+    partial = mm(dgate, w_cat[:, :inner], 1, 1) + mm(dpre * mine[None, :], w_cat[:, inner:], 1, 1)
+    grad_normed = pair_sum(partial.astype(BF16), "tp")
+    grad_gate = mm(normed, dgate, 0, 0).astype(BF16)
+    grad_rest = mm(normed, dpre, 0, 0).astype(BF16)
+    if last:
+        whole = jnp.concatenate([grad_gate, grad_rest, grad_out], axis=1)
+        shard = lax.psum_scatter(whole, ROWS, scatter_dimension=0, tiled=True).astype(F32)
+    else:
+        early = scattered(jnp.concatenate([grad_out, grad_gate], axis=1))
+        shard = jnp.concatenate(
+            [early[:, inner:], scattered(grad_rest), early[:, :inner]], axis=1
+        )
     scale = lax.rsqrt(jnp.mean(residual * residual, axis=1, keepdims=True) + EPSILON)
     grad_gain = jnp.sum(grad_normed * residual * scale, axis=0)
     pull = grad_normed * gain[None, :]
@@ -516,7 +603,7 @@
         ],
         axis=0,
     )
-    return (upstream, shards, small)
+    return (upstream, shard, small)
 
 
 def on_device(
@@ -546,7 +633,6 @@
     size = inner // head_count
     wide = inner + 2 * state
     dims = (tokens, inner, state, lags, size)
-    place = lax.axis_index("ctx")
 
     gathered = []
     for l in range(layer_count):
@@ -554,8 +640,13 @@
         packed = jnp.concatenate(
             [in_proj[l].reshape(rows, 2 * inner), state_proj[l], steps], axis=1
         )
-        w_cat = lax.all_gather(packed, ROWS, axis=0, tiled=True)
-        w_out = lax.all_gather(out_proj[l], ROWS, axis=0, tiled=True)
+        if l:
+            packed = jnp.concatenate([packed, out_proj[l]], axis=1)
+            packed = lax.all_gather(packed, ROWS, axis=0, tiled=True)
+            w_cat, w_out = (packed[:, : packed.shape[1] - inner], packed[:, -inner:])
+        else:
+            w_cat = lax.all_gather(packed, ROWS, axis=0, tiled=True)
+            w_out = doubled_gather(out_proj[l], bits("ctx")[::-1] + bits("fsdp"))
         gathered.append((w_cat, w_out))
 
     per_shard = norm_gain.shape[0]
@@ -600,9 +691,9 @@
     hide = jnp.where(visible, 0.0, HIDE).astype(F32)
 
     pairs = lax.axis_size("tp")
-    column = jnp.arange(2 * inner + 2 * state + LANES)
-    shared = (column >= 2 * inner) & (column < 2 * inner + 2 * state)
-    owner = (column - 2 * inner) * pairs // (2 * state)
+    column = jnp.arange(wide + LANES)
+    shared = (column >= inner) & (column < wide)
+    owner = (column - inner) * pairs // (2 * state)
     mine = (~shared | (owner == lax.axis_index("tp"))).astype(BF16)
 
     residual = hidden_in[0].astype(F32)
@@ -611,29 +702,27 @@
         taps = jnp.pad(flat[l, b:c].reshape(lags + 1, wide), ((0, 7 - lags), (0, 0)))
         params = (flat[l, :a].reshape(-1), taps, flat[l, c:], flat[l, a:b].reshape(-1), dims)
         residuals.append(residual)
-        residual, saved = layer_forward(residual, place, gathered[l], params, table, hide)
+        residual, saved = layer_forward(residual, gathered[l], params, table, hide)
         records.append(saved)
         layer_params.append(params)
     hidden_out = residual.astype(BF16)[None]
 
     upstream = cotangent[0].astype(F32)
-    cats, outs, smalls = ([None] * layer_count for _ in range(3))
+    shards, smalls = ([None] * layer_count, [None] * layer_count)
     for l in reversed(range(layer_count)):
-        upstream, shards, smalls[l] = layer_backward(
-            upstream, residuals[l], records[l], gathered[l], layer_params[l], table, hide, mine
+        upstream, shards[l], smalls[l] = layer_backward(
+            upstream, residuals[l], records[l], gathered[l], layer_params[l], table, hide, mine, l > 0
         )
-        cats[l], outs[l] = shards
-
-    cat = jnp.stack(cats, axis=0).astype(F32)
+
+    cat = jnp.stack(shards, axis=0)
     grad_in = cat[:, :, : 2 * inner].reshape(in_proj.shape)
     grad_state = cat[:, :, 2 * inner : 2 * inner + 2 * state]
     grad_step = cat[:, :, 2 * inner + 2 * state : 2 * inner + 2 * state + head_count]
-    grad_out = jnp.stack(outs, axis=0).astype(F32)
-
-    small = jnp.stack(smalls, axis=0)
-    pieces = lax.all_gather(small, ROWS)
+    grad_out = cat[:, :, -inner:]
+
+    small = exchanged_sum(jnp.stack(smalls, axis=0))
     first_layer = lax.axis_index("fsdp") * per_shard
-    small = jnp.sum(lax.dynamic_slice_in_dim(pieces, first_layer, per_shard, 1), axis=0)
+    small = lax.dynamic_slice_in_dim(small, first_layer, per_shard, 0)
     d = a + (lags + 1) * wide // LANES
     taps_out = small[:, a:d].reshape(per_shard, lags + 1, wide)
     heads_out = small[:, d : d + 3, :head_count]

time: 1060 us -> 594 us (0.56)
  waiting for transfers between devices: 786 us -> 250 us
  starting transfers between devices: 20.7 us -> 106 us
  local copies, waits for them, and re-layouts: 64.9 us -> 52.2 us
    reduce_scatter x4 -> x1, waiting for transfers between devices: 340 us -> 0.02 us  [layer_backward(): lax.psum_scatter(whole, ROWS, scatter_dimension=0, tiled=True).astype(F32)]
    all_gather x7 -> x1, waiting for transfers between devices: 293 us -> 58.1 us  [on_device(): packed = lax.all_gather(packed, ROWS, axis=0, tiled=True)]
    all_gather x2 -> x1, waiting for transfers between devices: 133 us -> 52.8 us  [on_device(): w_cat = lax.all_gather(packed, ROWS, axis=0, tiled=True)]
    ppermute x0 -> x24, waiting for transfers between devices: none -> 80.1 us  [partner(): lax.ppermute(block, axis, [(i, i ^ bit) for i in range(lax.axis_size(axis...]
    ppermute x0 -> x24, starting transfers between devices: none -> 54 us  [partner(): lax.ppermute(block, axis, [(i, i ^ bit) for i in range(lax.axis_size(axis...]
    ppermute x6 -> x18, waiting for transfers between devices: 8.68 us -> 54.2 us  [shifted(): return lax.ppermute(block, axis, route)]
    ppermute x6 -> x18, starting transfers between devices: 18.2 us -> 50.7 us  [shifted(): return lax.ppermute(block, axis, route)]
    unnamed x249 -> x171, local copies, waits for them, and re-layouts: 39.8 us -> 17.9 us
  transfers between devices with their start and end apart: 29 -> 55, of which waited for: 24 -> 28; matrix products, arithmetic and copies ran while one was open for 7% -> 15% of each run, Pallas kernels for 4% -> 10%
where the time goes in v2:
time: 594 us; the launch traced here: 585 us
  waiting for transfers between devices  250 us (42%)
  starting transfers between devices  106 us (18%)
  Pallas kernels  81.2 us (14%)
  local copies, waits for them, and re-layouts  52.2 us (9%)
  matrix products  37.6 us (6%)
  other arithmetic  36.3 us (6%)
  between operations  16.1 us (3%)
    pallas_call x18, Pallas kernels, call(): pl.pallas_call(functools.partial(kernel, dims), out_shape=shapes, in_spec...  81.2 us
    ppermute x24, waiting for transfers between devices, partner(): lax.ppermute(block, axis, [(i, i ^ bit) for i in range(lax.axis_size(axis...  80.1 us
    all_gather x1, waiting for transfers between devices, on_device(): packed = lax.all_gather(packed, ROWS, axis=0, tiled=True)  58.1 us
    ppermute x18, waiting for transfers between devices, shifted(): return lax.ppermute(block, axis, route)  54.2 us
    ppermute x24, starting transfers between devices, partner(): lax.ppermute(block, axis, [(i, i ^ bit) for i in range(lax.axis_size(axis...  54 us
    all_gather x1, waiting for transfers between devices, on_device(): w_cat = lax.all_gather(packed, ROWS, axis=0, tiled=True)  52.8 us
    ppermute x18, starting transfers between devices, shifted(): return lax.ppermute(block, axis, route)  50.7 us
    dot_general x16, matrix products, mm(): lax.dot_general(a, b, (((ca,), (cb,)), ((), ())), preferred_element_type=...  37.6 us
  transfers between devices with their start and end apart: 55, of which 28 were waited for; matrix products, arithmetic and copies ran while one was open for 15% of the time, Pallas kernels for 10%

profile of v2, /device:TPU:0, one launch (start us, length us, event | category | flops | bytes accessed | tf_op | source)
XLA Modules:
  0.0 584.7 jit_solution(8813108484594475214)
XLA Ops:
  12.3 4.1 collective-permute-start.7
  16.7 3.4 collective-permute-start
  21.5 4.5 collective-permute-start.1
  26.3 4.7 all_gather.9
  33.3 6.6 %collective-permute-done.8 = bf16[2,64,1024]{2,1,0:T(8,128)(2,1)S(1)} collective-permute-done((bf16[2,64,1024]{2,1,0:T(8,128)(2,1)S(1)}, bf16[2,64,1024]{2,1,0:T(8,128)(2,1)S(1)}, u32[]{:S(2)}, u32[]{:S(2)}) %collective-permute-start.8) | collective-permute-done | bytes 262176 | tf_op jit(solution)/shard_map/ppermute | solution.py:49
  48.8 13.6 %collective-permute-done.9 = bf16[2,2,64,1024]{3,2,1,0:T(8,128)(2,1)} collective-permute-done((bf16[2,2,64,1024]{3,2,1,0:T(8,128)(2,1)}, bf16[2,2,64,1024]{3,2,1,0:T(8,128)(2,1)}, u32[]{:S(2)}, u32[]{:S(2)}) %collective-permute-start.9) | collective-permute-done | bytes 524320 | tf_op jit(solution)/shard_map/ppermute | solution.py:49
  66.2 52.8 %all-gather.3.cloned.1.call-done = bf16[1024,2432]{1,0:T(8,128)(2,1)} async-done(((bf16[64,2432]{1,0:T(8,128)(2,1)}), bf16[1024,2432]{1,0:T(8,128)(2,1)}) %all-gather.3.cloned.1.call-update) | async-done | bytes 4980752 | tf_op jit(solution)/shard_map/all_gather | solution.py:648
  119.1 5.5 fusion.91.proj.gate
  124.6 7.0 %front_kernel.2 = (f32[256,1280]{1,0:T(8,128)S(1)}, f32[256,1280]{1,0:T(8,128)S(1)}, f32[256,1024]{1,0:T(8,128)S(1)}, f32[256,128]{1,0:T(8,128)S(1)}, f32[256,128]{1,0:T(8,128)S(1)}, /*index=5*/bf16[1040,128]{1,0:T(8,128)(2,1)}) custom-call(f32[264,2432]{1,0:T(8,128)} %fusion.91.proj.gate, f32[256,128]{1,0:T(8,128)S(1)} %stack.156.where_, ...), custom_call_target="tpu_custom_call" | custom-call | bytes 6942720 | tf_op jit(solution)/shard_map/front_kernel/pallas_call | solution.py:399
  133.3 3.9 collective-permute-start.3
  137.3 2.5 collective-permute-start.5
  139.8 3.3 collective-permute-done.3.refs_1_.refs_0_
  144.3 8.6 %collective-permute-start.4 = (bf16[1040,128]{1,0:T(8,128)(2,1)S(1)}, bf16[1040,128]{1,0:T(8,128)(2,1)S(1)}, u32[]{:S(2)}, u32[]{:S(2)}) collective-permute-start(bf16[1040,128]{1,0:T(8,128)(2,1)S(1)} %fold_kernel.4), channel_id=1, source_target_pairs={{0,4},{2,6},{4,8},{6,10},{8,12},{10,14},{1,5},{3,7},{5,9},{7,11},{... | collective-permute-start | bytes 798728 | tf_op jit(solution)/shard_map/ppermute | solution.py:26
  155.8 4.3 within_kernel.2.within
  160.1 2.7 collective-permute-done.4.refs_1_
  162.8 3.6 join_kernel.2
  169.0 2.7 collective-permute-done.11
  175.8 58.1 %all-gather.5.cloned.1.call-done = bf16[1024,3456]{1,0:T(8,128)(2,1)} async-done(((bf16[64,3456]{1,0:T(8,128)(2,1)}), bf16[1024,3456]{1,0:T(8,128)(2,1)}) %all-gather.5.cloned.1.call-update) | async-done | bytes 7077904 | tf_op jit(solution)/shard_map/all_gather | solution.py:645
  233.9 5.4 fusion.proj.gate
  239.3 6.3 %front_kernel.3 = (f32[256,1280]{1,0:T(8,128)S(1)}, f32[256,1280]{1,0:T(8,128)S(1)}, f32[256,1024]{1,0:T(8,128)S(1)}, f32[256,128]{1,0:T(8,128)S(1)}, f32[256,12...) custom-call(f32[264,2432]{1,0:T(8,128)} %fusion.proj.gate, f32[256,128]{1,0:T(8,128)S(1)} %stack.156.where_, ...), custom_call_target="tpu_custom_call" | custom-call | bytes 6942720 | tf_op jit(solution)/shard_map/front_kernel/pallas_call | solution.py:399
  245.7 2.7 collective-permute-start.13
  248.3 3.6 collective-permute-start.15
  252.8 7.0 %collective-permute-start.14 = (bf16[1040,128]{1,0:T(8,128)(2,1)S(1)}, bf16[1040,128]{1,0:T(8,128)(2,1)S(1)}, u32[]{:S(2)}, u32[]{:S(2)}) collective-permute-start(bf16[1040,128]{1,0:T(8,128)(2,1)S(1)} %fold_kernel.5), channel_id=1, source_target_pairs={{0,4},{2,6},{4,8},{6,10},{8,12},{10,14},{1,5},{3,7},{5,9},{7,11},{... | collective-permute-start | bytes 798728 | tf_op jit(solution)/shard_map/ppermute | solution.py:26
  259.8 4.3 within_kernel.3.within
  264.2 3.7 join_kernel.3
  267.9 4.3 multiply_reduce_fusion.9
  277.5 4.1 gate_back_kernel.2
  285.0 7.9 %within_back_kernel.2 = (f32[256,1024]{1,0:T(8,128)S(1)}, f32[256,256]{1,0:T(8,128)S(1)}) custom-call(f32[256,1280]{1,0:T(8,128)S(1)} %copy-done.5, f32[256,1024]{1,0:T(8,128)S(1)} %copy-done.17, f32[256,128]{1,0:T(8,128)S(1)} %get-tuple-element.67.cum, f32[256,256]{1,0:T(8,128)S(1)} %fusion.65.hide, f32[256,1024]{1,0:T(8,128)S(1)} %get-tuple-element.73.dy), custom_call_target="tpu_custom_call" | custom-call | flops 2000000000 | bytes 5111808 | tf_op jit(solution)/shard_map/within_back_kernel/pallas_call | solution.py:399
  292.9 4.0 collective-permute-done.19.refs_1_.refs_0_
  298.9 3.4 fusion.14
  302.2 9.7 %collective-permute-done.21.refs_2_ = bf16[1040,128]{1,0:T(8,128)(2,1)S(1)} collective-permute-done((bf16[1040,128]{1,0:T(8,128)(2,1)S(1)}, bf16[1040,128]{1,0:T(8,128)(2,1)S(1)}, u32[]{:S(2)}, u32[]{:S(2)}) %collective-permute-start.21) | collective-permute-done | bytes 266272 | tf_op jit(solution)/shard_map/ppermute | solution.py:26
  311.9 3.0 collective-permute-done.20.refs_1_
  314.9 10.2 %finish_kernel.2 = (f32[256,1024]{1,0:T(8,128)S(1)}, bf16[256,256]{1,0:T(8,128)(2,1)S(1)}, f32[256,128]{1,0:T(8,128)S(1)}, f32[8,128]{1,0:T(8,128)S(1)}) custom-call(f32[256,1024]{1,0:T(8,128)S(1)} %get-tuple-element.74.dxs_within, f32[256,256]{1,0:T(8,128)S(1)} %get-tuple-element.75.dmaps_within, f32[256,1024]{1,0:T(8,128)S(1)} %get-tuple-element.73.dy, ...), custom_call_target="tpu_custom_call" | custom-call | bytes 10248192 | tf_op jit(solution)/shard_map/finish_kernel/pallas_call | solution.py:399
  325.3 2.1 convert_bitcast_fusion
  332.9 4.0 copy.97
  339.0 2.9 conv_back_kernel.2
  344.4 3.3 pad_maximum_fusion
  348.8 2.9 fusion.4
  351.7 2.4 fusion.30
  357.0 3.4 multiply_subtract_fusion
  364.1 4.0 gate_back_kernel.3
  371.6 9.1 %collective-permute-done.26.refs_1_.refs_0_ = bf16[1040,128]{1,0:T(8,128)(2,1)S(1)} collective-permute-done((bf16[1040,128]{1,0:T(8,128)(2,1)S(1)}, bf16[1040,128]{1,0:T(8,128)(2,1)S(1)}, u32[]{:S(2)}, u32[]{:S(2)}) %collective-permute-start.26) | collective-permute-done | bytes 266272 | tf_op jit(solution)/shard_map/ppermute | solution.py:26
  386.3 7.9 %within_back_kernel.3 = (f32[256,1024]{1,0:T(8,128)S(1)}, f32[256,256]{1,0:T(8,128)S(1)}) custom-call(f32[256,1280]{1,0:T(8,128)S(1)} %copy-done.3, f32[256,1024]{1,0:T(8,128)S(1)} %copy-done.13, f32[256,128]{1,0:T(8,128)S(1)} %get-tuple-element.61.cum, f32[256,256]{1,0:T(8,128)S(1)} %fusion.65.hide, f32[256,1024]{1,0:T(8,128)S(1)} %get-tuple-element.86.dy), custom_call_target="tpu_custom_call" | custom-call | flops 2000000000 | bytes 5111808 | tf_op jit(solution)/shard_map/within_back_kernel/pallas_call | solution.py:399
  394.2 20.4 %collective-permute-done.28.refs_2_ = bf16[1040,128]{1,0:T(8,128)(2,1)S(1)} collective-permute-done((bf16[1040,128]{1,0:T(8,128)(2,1)S(1)}, bf16[1040,128]{1,0:T(8,128)(2,1)S(1)}, u32[]{:S(2)}, u32[]{:S(2)}) %collective-permute-start.28) | collective-permute-done | bytes 266272 | tf_op jit(solution)/shard_map/ppermute | solution.py:26
  414.6 10.3 %finish_kernel.3 = (f32[256,1024]{1,0:T(8,128)S(1)}, bf16[256,256]{1,0:T(8,128)(2,1)S(1)}, f32[256,128]{1,0:T(8,128)S(1)}, f32[8,128]{1,0:T(8,128)S(1)}) custom-call(f32[256,1024]{1,0:T(8,128)S(1)} %get-tuple-element.87.dxs_within, f32[256,256]{1,0:T(8,128)S(1)} %get-tuple-element.88.dmaps_within, f32[256,1024]{1,0:T(8,128)S(1)} %get-tuple-element.86.dy, ...), custom_call_target="tpu_custom_call" | custom-call | bytes 10248192 | tf_op jit(solution)/shard_map/finish_kernel/pallas_call | solution.py:399
  431.2 5.2 collective-permute-start.36
  436.4 2.9 conv_back_kernel.3
  443.0 3.3 fusion.27
  446.5 6.4 %collective-permute-start.44 = (bf16[2,2,2,64,768]{4,3,1,2,0:T(8,128)(2,1)S(1)}, bf16[2,2,2,64,768]{4,3,1,2,0:T(8,128)(2,1)S(1)}, u32[]{:S(2)}, u32[]{:S(2)}) collective-permute-start(bf16[2,2,2,64,768]{4,3,1,2,0:T(8,128)(2,1)S(1)} %bitcast.268), channel_id=1, source_target_pairs={{0,2},{2,0},{4,6},{6,4},{8,10},{10,8},{12,14},{14,12},{1,3},{3,1},... | collective-permute-start | bytes 2359304 | tf_op jit(solution)/shard_map/ppermute | solution.py:49
  458.5 8.9 %collective-permute-done.36 = bf16[2,2,2,64,1024]{4,3,1,2,0:T(8,128)(2,1)} collective-permute-done((bf16[2,2,2,64,1024]{4,3,1,2,0:T(8,128)(2,1)}, bf16[2,2,2,64,1024]{4,3,1,2,0:T(8,128)(2,1)}, u32[]{:S(2)}, u32[]{:S(2)}) %collective-permute-start.36) | collective-permute-done | bytes 1048608 | tf_op jit(solution)/shard_map/ppermute | solution.py:49
  474.0 2.5 subtract_bitcast_fusion
  476.5 20.4 %collective-permute-done.32 = f32[2,69,128]{2,1,0:T(8,128)S(1)} collective-permute-done((f32[2,69,128]{2,1,0:T(8,128)S(1)}, f32[2,69,128]{2,1,0:T(8,128)S(1)}, u32[]{:S(2)}, u32[]{:S(2)}) %collective-permute-start.32) | collective-permute-done | bytes 70688 | tf_op jit(solution)/shard_map/ppermute | solution.py:49
  496.9 4.2 collective-permute-start.33
  501.3 7.8 %collective-permute-done.33 = f32[2,69,128]{2,1,0:T(8,128)S(1)} collective-permute-done((f32[2,69,128]{2,1,0:T(8,128)S(1)}, f32[2,69,128]{2,1,0:T(8,128)S(1)}, u32[]{:S(2)}, u32[]{:S(2)}) %collective-permute-start.33) | collective-permute-done | bytes 70688 | tf_op jit(solution)/shard_map/ppermute | solution.py:49
  511.0 2.5 collective-permute-done.34
  517.0 5.1 collective-permute-done.35
  533.8 2.3 collective-permute-start.50
  540.6 3.4 collective-permute-done.50
  544.1 3.2 collective-permute-start.51
  548.3 4.6 collective-permute-start.39
  553.0 4.1 collective-permute-start.43
  558.3 2.7 collective-permute-start.46
  561.0 2.5 collective-permute-done.43
  566.0 6.4 %collective-permute-done.47 = bf16[64,768]{1,0:T(8,128)(2,1)S(1)} collective-permute-done((bf16[64,768]{1,0:T(8,128)(2,1)S(1)}, bf16[64,768]{1,0:T(8,128)(2,1)S(1)}, u32[]{:S(2)}, u32[]{:S(2)}) %collective-permute-start.47) | collective-permute-done | bytes 98336 | tf_op jit(solution)/shard_map/ppermute | solution.py:49
  (410 shorter events, 126.1 us)
Async XLA Ops:
  7.2 111.9 %all-gather.3.cloned.1.call-start = ((), (), s32[]{:S(2)}) async-start(), calls=%async_computation.1 | async-start | bytes 5292032 | tf_op jit(solution)/shard_map/all_gather | solution.py:648
  11.1 222.8 %all-gather.5.cloned.1.call-start = ((), (), s32[]{:S(2)}) async-start(), calls=%async_computation.2 | async-start | bytes 7520256 | tf_op jit(solution)/shard_map/all_gather | solution.py:645
  12.3 560.2 %reduce-scatter.2.cloned.1.call-start = ((), (), s32[]{:S(2)}) async-start(), calls=%async_computation.3 | async-start | bytes 7520256 | tf_op jit(solution)/shard_map/reduce_scatter | solution.py:586
  12.3 18.6 %collective-permute-start.7 = (bf16[64,1024]{1,0:T(8,128)(2,1)S(1)}, bf16[64,1024]{1,0:T(8,128)(2,1)S(1)}, u32[]{:S(2)}, u32[]{:S(2)}) collective-permute-start(bf16[64,1024]{1,0:T(8,128)(2,1)S(1)} %get-tuple-element.180), channel_id=1, source_target_pairs={{0,8},{2,10},{4,12},{6,14},{8,0},{10,2},{12,4},{14,6},{1,9},{3,11}... | collective-permute-start | bytes 393224 | tf_op jit(solution)/shard_map/ppermute | solution.py:49
  16.7 31.9 %collective-permute-start = (f32[8,1024]{1,0:T(8,128)S(1)}, f32[8,1024]{1,0:T(8,128)S(1)}, u32[]{:S(2)}, u32[]{:S(2)}) collective-permute-start(f32[8,1024]{1,0:T(8,128)S(1)} %slice_bitcast_fusion.2), channel_id=1, source_target_pairs={{0,2},{2,4},{4,6},{6,8},{8,10},{10,12},{12,14},{1,3},{3,5},{5,7},{... | collective-permute-start | bytes 98312 | tf_op jit(solution)/shard_map/ppermute | solution.py:26
  20.2 22.2 %collective-permute-start.2 = (s32[8]{0:T(128)S(1)}, s32[8]{0:T(128)S(1)}, u32[]{:S(2)}, u32[]{:S(2)}) collective-permute-start(s32[8]{0:T(128)S(1)} %get-tuple-element.211), channel_id=1, source_target_pairs={{2,0},{4,2},{6,4},{8,6},{10,8},{12,10},{14,12},{3,1},{5,3},{7,5},{... | collective-permute-start | bytes 104 | tf_op jit(solution)/shard_map/ppermute | solution.py:26
  21.5 20.9 %collective-permute-start.1 = (s32[8]{0:T(128)S(1)}, s32[8]{0:T(128)S(1)}, u32[]{:S(2)}, u32[]{:S(2)}) collective-permute-start(s32[8]{0:T(128)S(1)} %get-tuple-element.212), channel_id=1, source_target_pairs={{0,2},{2,4},{4,6},{6,8},{8,10},{10,12},{12,14},{1,3},{3,5},{5,7},{... | collective-permute-start | bytes 104 | tf_op jit(solution)/shard_map/ppermute | solution.py:26
  31.0 8.8 %collective-permute-start.8 = (bf16[2,64,1024]{2,1,0:T(8,128)(2,1)S(1)}, bf16[2,64,1024]{2,1,0:T(8,128)(2,1)S(1)}, u32[]{:S(2)}, u32[]{:S(2)}) collective-permute-start(bf16[2,64,1024]{2,1,0:T(8,128)(2,1)S(1)} %pad_maximum_fusion.7), channel_id=1, source_target_pairs={{0,4},{2,6},{4,0},{6,2},{8,12},{10,14},{12,8},{14,10},{1,5},{3,7},... | collective-permute-start | bytes 786440 | tf_op jit(solution)/shard_map/ppermute | solution.py:49
  40.7 21.7 %collective-permute-start.9 = (bf16[2,2,64,1024]{3,2,1,0:T(8,128)(2,1)}, bf16[2,2,64,1024]{3,2,1,0:T(8,128)(2,1)}, u32[]{:S(2)}, u32[]{:S(2)}) collective-permute-start(bf16[2,2,64,1024]{3,2,1,0:T(8,128)(2,1)} %pad_maximum_fusion.6), channel_id=1, source_target_pairs={{0,2},{2,0},{4,6},{6,4},{8,10},{10,8},{12,14},{14,12},{1,3},{3,1},... | collective-permute-start | bytes 1572872 | tf_op jit(solution)/shard_map/ppermute | solution.py:49
  63.6 61.0 %copy-start.56 = (bf16[2,2,1,64,1024]{4,3,2,1,0:T(8,128)(2,1)}, bf16[2,2,1,64,1024]{4,3,2,1,0:T(8,128)(2,1)S(1)}, u32[]{:S(2)}) copy-start(bf16[2,2,1,64,1024]{4,3,2,1,0:T(8,128)(2,1)S(1)} %get-tuple-element.169) | copy-start | bytes 1572868
  64.7 88.1 %collective-permute-start.10 = (bf16[2,2,2,64,1024]{4,3,2,1,0:T(8,128)(2,1)}, bf16[2,2,2,64,1024]{4,3,2,1,0:T(8,128)(2,1)}, u32[]{:S(2)}, u32[]{:S(2)}) collective-permute-start(bf16[2,2,2,64,1024]{4,3,2,1,0:T(8,128)(2,1)} %pad_maximum_fusion.4), channel_id=1, source_target_pairs={{0,16},{16,0},{1,17},{17,1},{2,18},{18,2},{3,19},{19,3},{4,20},{20... | collective-permute-start | bytes 3145736 | tf_op jit(solution)/shard_map/ppermute | solution.py:49
  66.2 58.3 %copy-start.50 = (bf16[264,1024]{1,0:T(8,128)(2,1)}, bf16[264,1024]{1,0:T(8,128)(2,1)S(1)}, u32[]{:S(2)}) copy-start(bf16[264,1024]{1,0:T(8,128)(2,1)S(1)} %multiply_convert_fusion.1) | copy-start | bytes 1622020
  133.3 21.3 %copy-start.11 = (f32[256,1024]{1,0:T(8,128)}, f32[256,1024]{1,0:T(8,128)S(1)}, u32[]{:S(2)}) copy-start(f32[256,1024]{1,0:T(8,128)S(1)} %get-tuple-element.60.xs) | copy-start | bytes 3145732
  133.3 29.6 %copy-start.2 = (f32[256,1280]{1,0:T(8,128)}, f32[256,1280]{1,0:T(8,128)S(1)}, u32[]{:S(2)}) copy-start(f32[256,1280]{1,0:T(8,128)S(1)} %get-tuple-element.59.act) | copy-start | bytes 3932164
  133.3 9.8 %collective-permute-start.3 = (bf16[1040,128]{1,0:T(8,128)(2,1)}, bf16[1040,128]{1,0:T(8,128)(2,1)S(1)}, u32[]{:S(2)}, u32[]{:S(2)}) collective-permute-start(bf16[1040,128]{1,0:T(8,128)(2,1)} %get-tuple-element.62.refs_0_), channel_id=1, source_target_pairs={{0,2},{2,4},{4,6},{6,8},{8,10},{10,12},{12,14},{1,3},{3,5},{5,7},{... | collective-permute-start | bytes 798728 | tf_op jit(solution)/shard_map/ppermute | solution.py:26
  137.3 22.8 %collective-permute-start.5 = (bf16[1040,128]{1,0:T(8,128)(2,1)}, bf16[1040,128]{1,0:T(8,128)(2,1)S(1)}, u32[]{:S(2)}, u32[]{:S(2)}) collective-permute-start(bf16[1040,128]{1,0:T(8,128)(2,1)} %get-tuple-element.62.refs_0_), channel_id=1, source_target_pairs={{0,8},{2,10},{4,12},{6,14},{1,9},{3,11},{5,13},{7,15},{16,24},{18,... | collective-permute-start | bytes 798728 | tf_op jit(solution)/shard_map/ppermute | solution.py:26
  144.3 18.5 %collective-permute-start.4 = (bf16[1040,128]{1,0:T(8,128)(2,1)S(1)}, bf16[1040,128]{1,0:T(8,128)(2,1)S(1)}, u32[]{:S(2)}, u32[]{:S(2)}) collective-permute-start(bf16[1040,128]{1,0:T(8,128)(2,1)S(1)} %fold_kernel.4), channel_id=1, source_target_pairs={{0,4},{2,6},{4,8},{6,10},{8,12},{10,14},{1,5},{3,7},{5,9},{7,11},{... | collective-permute-start | bytes 798728 | tf_op jit(solution)/shard_map/ppermute | solution.py:26
  166.4 1.2 collective-permute-start.6
  169.0 2.7 collective-permute-start.11
  172.6 66.7 %copy-start.37 = (f32[256,1024]{1,0:T(8,128)}, f32[256,1024]{1,0:T(8,128)S(1)}, u32[]{:S(2)}) copy-start(f32[256,1024]{1,0:T(8,128)S(1)} %get-tuple-element.153) | copy-start | bytes 3145732
  172.6 2.9 collective-permute-start.12
  175.8 63.5 %copy-start.52 = (bf16[264,1024]{1,0:T(8,128)(2,1)}, bf16[264,1024]{1,0:T(8,128)(2,1)S(1)}, u32[]{:S(2)}) copy-start(bf16[264,1024]{1,0:T(8,128)(2,1)S(1)} %multiply_convert_fusion) | copy-start | bytes 1622020
  245.7 6.9 %collective-permute-start.13 = (bf16[1040,128]{1,0:T(8,128)(2,1)S(1)}, bf16[1040,128]{1,0:T(8,128)(2,1)S(1)}, u32[]{:S(2)}, u32[]{:S(2)}) collective-permute-start(bf16[1040,128]{1,0:T(8,128)(2,1)S(1)} %get-tuple-element.68.refs_0_), channel_id=1, source_target_pairs={{0,2},{2,4},{4,6},{6,8},{8,10},{10,12},{12,14},{1,3},{3,5},{5,7},{... | collective-permute-start | bytes 798728 | tf_op jit(solution)/shard_map/ppermute | solution.py:26
  248.3 15.8 %collective-permute-start.15 = (bf16[1040,128]{1,0:T(8,128)(2,1)S(1)}, bf16[1040,128]{1,0:T(8,128)(2,1)S(1)}, u32[]{:S(2)}, u32[]{:S(2)}) collective-permute-start(bf16[1040,128]{1,0:T(8,128)(2,1)S(1)} %get-tuple-element.68.refs_0_), channel_id=1, source_target_pairs={{0,8},{2,10},{4,12},{6,14},{1,9},{3,11},{5,13},{7,15},{16,24},{18,... | collective-permute-start | bytes 798728 | tf_op jit(solution)/shard_map/ppermute | solution.py:26
  252.8 11.3 %collective-permute-start.14 = (bf16[1040,128]{1,0:T(8,128)(2,1)S(1)}, bf16[1040,128]{1,0:T(8,128)(2,1)S(1)}, u32[]{:S(2)}, u32[]{:S(2)}) collective-permute-start(bf16[1040,128]{1,0:T(8,128)(2,1)S(1)} %fold_kernel.5), channel_id=1, source_target_pairs={{0,4},{2,6},{4,8},{6,10},{8,12},{10,14},{1,5},{3,7},{5,9},{7,11},{... | collective-permute-start | bytes 798728 | tf_op jit(solution)/shard_map/ppermute | solution.py:26
  272.2 1.2 collective-permute-start.18
  272.3 1.3 collective-permute-start.16
  281.5 49.3 %copy-start.31 = (bf16[256,1024]{1,0:T(8,128)(2,1)}, bf16[256,1024]{1,0:T(8,128)(2,1)S(1)}, u32[]{:S(2)}) copy-start(bf16[256,1024]{1,0:T(8,128)(2,1)S(1)} %get-tuple-element.72) | copy-start | bytes 1572868
  281.6 15.4 %collective-permute-start.19 = (bf16[1040,128]{1,0:T(8,128)(2,1)S(1)}, bf16[1040,128]{1,0:T(8,128)(2,1)S(1)}, u32[]{:S(2)}, u32[]{:S(2)}) collective-permute-start(bf16[1040,128]{1,0:T(8,128)(2,1)S(1)} %get-tuple-element.79.refs_0_), channel_id=1, source_target_pairs={{2,0},{4,2},{6,4},{8,6},{10,8},{12,10},{14,12},{3,1},{5,3},{7,5},{... | collective-permute-start | bytes 798728 | tf_op jit(solution)/shard_map/ppermute | solution.py:26
  283.5 28.4 %collective-permute-start.21 = (bf16[1040,128]{1,0:T(8,128)(2,1)S(1)}, bf16[1040,128]{1,0:T(8,128)(2,1)S(1)}, u32[]{:S(2)}, u32[]{:S(2)}) collective-permute-start(bf16[1040,128]{1,0:T(8,128)(2,1)S(1)} %get-tuple-element.79.refs_0_), channel_id=1, source_target_pairs={{8,0},{10,2},{12,4},{14,6},{9,1},{11,3},{13,5},{15,7},{24,16},{26,... | collective-permute-start | bytes 798728 | tf_op jit(solution)/shard_map/ppermute | solution.py:26
  297.2 17.7 %collective-permute-start.20 = (bf16[1040,128]{1,0:T(8,128)(2,1)S(1)}, bf16[1040,128]{1,0:T(8,128)(2,1)S(1)}, u32[]{:S(2)}, u32[]{:S(2)}) collective-permute-start(bf16[1040,128]{1,0:T(8,128)(2,1)S(1)} %fold_kernel.6), channel_id=1, source_target_pairs={{4,0},{6,2},{8,4},{10,6},{12,8},{14,10},{5,1},{7,3},{9,5},{11,7},{... | collective-permute-start | bytes 798728 | tf_op jit(solution)/shard_map/ppermute | solution.py:26
  325.2 2.7 collective-permute-start.22
  327.4 29.6 %collective-permute-start.17 = (f32[256,1024]{1,0:T(8,128)}, f32[256,1024]{1,0:T(8,128)}, u32[]{:S(2)}, u32[]{:S(2)}) collective-permute-start(f32[256,1024]{1,0:T(8,128)} %fusion.14), channel_id=1, source_target_pairs={{0,1},{1,0},{2,3},{3,2},{4,5},{5,4},{6,7},{7,6},{8,9},{9,8},{10,11... | collective-permute-start | bytes 3145736 | tf_op jit(solution)/shard_map/ppermute | solution.py:31
  329.0 7.8 %collective-permute-start.23 = (f32[8,1280]{1,0:T(8,128)S(1)}, f32[8,1280]{1,0:T(8,128)S(1)}, u32[]{:S(2)}, u32[]{:S(2)}) collective-permute-start(f32[8,1280]{1,0:T(8,128)S(1)} %pad_maximum_fusion.11), channel_id=1, source_target_pairs={{2,0},{4,2},{6,4},{8,6},{10,8},{12,10},{14,12},{3,1},{5,3},{7,5},{... | collective-permute-start | bytes 122888 | tf_op jit(solution)/shard_map/ppermute | solution.py:26
  354.2 2.0 collective-permute-start.24
  361.4 1.3 collective-permute-start.25
  368.2 12.6 %collective-permute-start.26 = (bf16[1040,128]{1,0:T(8,128)(2,1)S(1)}, bf16[1040,128]{1,0:T(8,128)(2,1)S(1)}, u32[]{:S(2)}, u32[]{:S(2)}) collective-permute-start(bf16[1040,128]{1,0:T(8,128)(2,1)S(1)} %get-tuple-element.92.refs_0_), channel_id=1, source_target_pairs={{2,0},{4,2},{6,4},{8,6},{10,8},{12,10},{14,12},{3,1},{5,3},{7,5},{... | collective-permute-start | bytes 798728 | tf_op jit(solution)/shard_map/ppermute | solution.py:26
  370.3 44.3 %collective-permute-start.28 = (bf16[1040,128]{1,0:T(8,128)(2,1)S(1)}, bf16[1040,128]{1,0:T(8,128)(2,1)S(1)}, u32[]{:S(2)}, u32[]{:S(2)}) collective-permute-start(bf16[1040,128]{1,0:T(8,128)(2,1)S(1)} %get-tuple-element.92.refs_0_), channel_id=1, source_target_pairs={{8,0},{10,2},{12,4},{14,6},{9,1},{11,3},{13,5},{15,7},{24,16},{26,... | collective-permute-start | bytes 798728 | tf_op jit(solution)/shard_map/ppermute | solution.py:26
  381.0 33.6 %collective-permute-start.27 = (bf16[1040,128]{1,0:T(8,128)(2,1)S(1)}, bf16[1040,128]{1,0:T(8,128)(2,1)S(1)}, u32[]{:S(2)}, u32[]{:S(2)}) collective-permute-start(bf16[1040,128]{1,0:T(8,128)(2,1)S(1)} %fold_kernel.7), channel_id=1, source_target_pairs={{4,0},{6,2},{8,4},{10,6},{12,8},{14,10},{5,1},{7,3},{9,5},{11,7},{... | collective-permute-start | bytes 798728 | tf_op jit(solution)/shard_map/ppermute | solution.py:26
  384.8 70.0 %collective-permute-start.48 = (bf16[2,2,2,64,1024]{4,3,0,1,2:T(8,128)(2,1)}, bf16[2,2,2,64,1024]{4,3,0,1,2:T(8,128)(2,1)}, u32[]{:S(2)}, u32[]{:S(2)}) collective-permute-start(bf16[2,2,2,64,1024]{4,3,0,1,2:T(8,128)(2,1)} %bitcast.246), channel_id=1, source_target_pairs={{0,16},{16,0},{1,17},{17,1},{2,18},{18,2},{3,19},{19,3},{4,20},{20... | collective-permute-start | bytes 3145736 | tf_op jit(solution)/shard_map/ppermute | solution.py:49
  386.3 28.3 %copy-start.28 = (f32[1024,128]{1,0:T(8,128)S(1)}, f32[1024,128]{1,0:T(8,128)}, u32[]{:S(2)}) copy-start(f32[1024,128]{1,0:T(8,128)} %copy-done.27) | copy-start | bytes 1572868
  386.3 28.3 %copy-start.34 = (f32[256,128]{1,0:T(8,128)S(1)}, f32[256,128]{1,0:T(8,128)}, u32[]{:S(2)}) copy-start(f32[256,128]{1,0:T(8,128)} %copy-done.33) | copy-start | bytes 393220
  424.9 1.4 collective-permute-start.29
  427.4 8.9 %collective-permute-start.30 = (f32[8,1280]{1,0:T(8,128)S(1)}, f32[8,1280]{1,0:T(8,128)S(1)}, u32[]{:S(2)}, u32[]{:S(2)}) collective-permute-start(f32[8,1280]{1,0:T(8,128)S(1)} %pad_maximum_fusion.12), channel_id=1, source_target_pairs={{2,0},{4,2},{6,4},{8,6},{10,8},{12,10},{14,12},{3,1},{5,3},{7,5},{... | collective-permute-start | bytes 122888 | tf_op jit(solution)/shard_map/ppermute | solution.py:26
  431.2 36.2 %collective-permute-start.36 = (bf16[2,2,2,64,1024]{4,3,1,2,0:T(8,128)(2,1)}, bf16[2,2,2,64,1024]{4,3,1,2,0:T(8,128)(2,1)}, u32[]{:S(2)}, u32[]{:S(2)}) collective-permute-start(bf16[2,2,2,64,1024]{4,3,1,2,0:T(8,128)(2,1)} %bitcast.247), channel_id=1, source_target_pairs={{0,2},{2,0},{4,6},{6,4},{8,10},{10,8},{12,14},{14,12},{1,3},{3,1},... | collective-permute-start | bytes 3145736 | tf_op jit(solution)/shard_map/ppermute | solution.py:49
  446.3 25.3 %collective-permute-start.31 = (bf16[256,1024]{1,0:T(8,128)(2,1)}, bf16[256,1024]{1,0:T(8,128)(2,1)}, u32[]{:S(2)}, u32[]{:S(2)}) collective-permute-start(bf16[256,1024]{1,0:T(8,128)(2,1)} %fusion.27), channel_id=1, source_target_pairs={{0,1},{1,0},{2,3},{3,2},{4,5},{5,4},{6,7},{7,6},{8,9},{9,8},{10,11... | collective-permute-start | bytes 1572872 | tf_op jit(solution)/shard_map/ppermute | solution.py:31
  446.5 68.1 %collective-permute-start.44 = (bf16[2,2,2,64,768]{4,3,1,2,0:T(8,128)(2,1)S(1)}, bf16[2,2,2,64,768]{4,3,1,2,0:T(8,128)(2,1)S(1)}, u32[]{:S(2)}, u32[]{:S(2)}) collective-permute-start(bf16[2,2,2,64,768]{4,3,1,2,0:T(8,128)(2,1)S(1)} %bitcast.268), channel_id=1, source_target_pairs={{0,2},{2,0},{4,6},{6,4},{8,10},{10,8},{12,14},{14,12},{1,3},{3,1},... | collective-permute-start | bytes 2359304 | tf_op jit(solution)/shard_map/ppermute | solution.py:49
  453.1 48.0 %collective-permute-start.40 = (bf16[2,2,2,64,640]{4,3,0,1,2:T(8,128)(2,1)S(1)}, bf16[2,2,2,64,640]{4,3,0,1,2:T(8,128)(2,1)S(1)}, u32[]{:S(2)}, u32[]{:S(2)}) collective-permute-start(bf16[2,2,2,64,640]{4,3,0,1,2:T(8,128)(2,1)S(1)} %bitcast.269), channel_id=1, source_target_pairs={{0,16},{16,0},{1,17},{17,1},{2,18},{18,2},{3,19},{19,3},{4,20},{20... | collective-permute-start | bytes 1966088 | tf_op jit(solution)/shard_map/ppermute | solution.py:49
  457.4 75.1 %collective-permute-start.49 = (bf16[2,2,64,1024]{3,2,0,1:T(8,128)(2,1)}, bf16[2,2,64,1024]{3,2,0,1:T(8,128)(2,1)}, u32[]{:S(2)}, u32[]{:S(2)}) collective-permute-start(bf16[2,2,64,1024]{3,2,0,1:T(8,128)(2,1)} %dynamic-slice_bitcast_fusion), channel_id=1, source_target_pairs={{0,2},{2,0},{4,6},{6,4},{8,10},{10,8},{12,14},{14,12},{1,3},{3,1},... | collective-permute-start | bytes 1572872 | tf_op jit(solution)/shard_map/ppermute | solution.py:49
  470.0 66.1 %collective-permute-start.37 = (bf16[2,2,64,1024]{3,2,0,1:T(8,128)(2,1)}, bf16[2,2,64,1024]{3,2,0,1:T(8,128)(2,1)}, u32[]{:S(2)}, u32[]{:S(2)}) collective-permute-start(bf16[2,2,64,1024]{3,2,0,1:T(8,128)(2,1)} %dynamic-slice_bitcast_fusion.1), channel_id=1, source_target_pairs={{0,16},{16,0},{1,17},{17,1},{2,18},{18,2},{3,19},{19,3},{4,20},{20... | collective-permute-start | bytes 1572872 | tf_op jit(solution)/shard_map/ppermute | solution.py:49
  473.3 23.6 %collective-permute-start.32 = (f32[2,69,128]{2,1,0:T(8,128)S(1)}, f32[2,69,128]{2,1,0:T(8,128)S(1)}, u32[]{:S(2)}, u32[]{:S(2)}) collective-permute-start(f32[2,69,128]{2,1,0:T(8,128)S(1)} %pad_maximum_fusion.8), channel_id=1, source_target_pairs={{0,16},{16,0},{1,17},{17,1},{2,18},{18,2},{3,19},{19,3},{4,20},{20... | collective-permute-start | bytes 211976 | tf_op jit(solution)/shard_map/ppermute | solution.py:49
  496.9 12.1 %collective-permute-start.33 = (f32[2,69,128]{2,1,0:T(8,128)S(1)}, f32[2,69,128]{2,1,0:T(8,128)S(1)}, u32[]{:S(2)}, u32[]{:S(2)}) collective-permute-start(f32[2,69,128]{2,1,0:T(8,128)S(1)} %fusion.84), channel_id=1, source_target_pairs={{0,8},{2,10},{4,12},{6,14},{8,0},{10,2},{12,4},{14,6},{1,9},{3,11}... | collective-permute-start | bytes 211976 | tf_op jit(solution)/shard_map/ppermute | solution.py:49
  509.1 4.4 collective-permute-start.34
  509.9 27.6 %collective-permute-start.41 = (bf16[2,2,64,640]{3,2,0,1:T(8,128)(2,1)}, bf16[2,2,64,640]{3,2,0,1:T(8,128)(2,1)}, u32[]{:S(2)}, u32[]{:S(2)}) collective-permute-start(bf16[2,2,64,640]{3,2,0,1:T(8,128)(2,1)} %dynamic-slice_bitcast_fusion.3), channel_id=1, source_target_pairs={{0,2},{2,0},{4,6},{6,4},{8,10},{10,8},{12,14},{14,12},{1,3},{3,1},... | collective-permute-start | bytes 983048 | tf_op jit(solution)/shard_map/ppermute | solution.py:49
  513.5 8.6 %collective-permute-start.35 = (f32[2,69,128]{2,1,0:T(8,128)S(1)}, f32[2,69,128]{2,1,0:T(8,128)S(1)}, u32[]{:S(2)}, u32[]{:S(2)}) collective-permute-start(f32[2,69,128]{2,1,0:T(8,128)S(1)} %add.324), channel_id=1, source_target_pairs={{0,2},{2,0},{4,6},{6,4},{8,10},{10,8},{12,14},{14,12},{1,3},{3,1},... | collective-permute-start | bytes 211976 | tf_op jit(solution)/shard_map/ppermute | solution.py:49
  515.6 41.6 %collective-permute-start.45 = (bf16[2,2,64,768]{3,2,0,1:T(8,128)(2,1)}, bf16[2,2,64,768]{3,2,0,1:T(8,128)(2,1)}, u32[]{:S(2)}, u32[]{:S(2)}) collective-permute-start(bf16[2,2,64,768]{3,2,0,1:T(8,128)(2,1)} %dynamic-slice_bitcast_fusion.2), channel_id=1, source_target_pairs={{0,16},{16,0},{1,17},{17,1},{2,18},{18,2},{3,19},{19,3},{4,20},{20... | collective-permute-start | bytes 1179656 | tf_op jit(solution)/shard_map/ppermute | solution.py:49
  533.8 10.2 %collective-permute-start.50 = (bf16[2,64,1024]{2,1,0:T(8,128)(2,1)S(1)}, bf16[2,64,1024]{2,1,0:T(8,128)(2,1)S(1)}, u32[]{:S(2)}, u32[]{:S(2)}) collective-permute-start(bf16[2,64,1024]{2,1,0:T(8,128)(2,1)S(1)} %dynamic-slice_bitcast_fusion.4), channel_id=1, source_target_pairs={{0,4},{2,6},{4,0},{6,2},{8,12},{10,14},{12,8},{14,10},{1,5},{3,7},... | collective-permute-start | bytes 786440 | tf_op jit(solution)/shard_map/ppermute | solution.py:49
  537.4 10.9 %collective-permute-start.38 = (bf16[2,64,1024]{2,1,0:T(8,128)(2,1)S(1)}, bf16[2,64,1024]{2,1,0:T(8,128)(2,1)S(1)}, u32[]{:S(2)}, u32[]{:S(2)}) collective-permute-start(bf16[2,64,1024]{2,1,0:T(8,128)(2,1)S(1)} %dynamic-slice_bitcast_fusion.5), channel_id=1, source_target_pairs={{0,4},{2,6},{4,0},{6,2},{8,12},{10,14},{12,8},{14,10},{1,5},{3,7},... | collective-permute-start | bytes 786440 | tf_op jit(solution)/shard_map/ppermute | solution.py:49
  538.5 14.4 %collective-permute-start.42 = (bf16[2,64,640]{2,1,0:T(8,128)(2,1)S(1)}, bf16[2,64,640]{2,1,0:T(8,128)(2,1)S(1)}, u32[]{:S(2)}, u32[]{:S(2)}) collective-permute-start(bf16[2,64,640]{2,1,0:T(8,128)(2,1)S(1)} %dynamic-slice_bitcast_fusion.7), channel_id=1, source_target_pairs={{0,4},{2,6},{4,0},{6,2},{8,12},{10,14},{12,8},{14,10},{1,5},{3,7},... | collective-permute-start | bytes 491528 | tf_op jit(solution)/shard_map/ppermute | solution.py:49
  544.1 19.4 %collective-permute-start.51 = (bf16[64,1024]{1,0:T(8,128)(2,1)S(1)}, bf16[64,1024]{1,0:T(8,128)(2,1)S(1)}, u32[]{:S(2)}, u32[]{:S(2)}) collective-permute-start(bf16[64,1024]{1,0:T(8,128)(2,1)S(1)} %dynamic-slice_bitcast_fusion.8), channel_id=1, source_target_pairs={{0,8},{2,10},{4,12},{6,14},{8,0},{10,2},{12,4},{14,6},{1,9},{3,11}... | collective-permute-start | bytes 393224 | tf_op jit(solution)/shard_map/ppermute | solution.py:49
  548.3 17.6 %collective-permute-start.39 = (bf16[64,1024]{1,0:T(8,128)(2,1)S(1)}, bf16[64,1024]{1,0:T(8,128)(2,1)S(1)}, u32[]{:S(2)}, u32[]{:S(2)}) collective-permute-start(bf16[64,1024]{1,0:T(8,128)(2,1)S(1)} %dynamic-slice_bitcast_fusion.9), channel_id=1, source_target_pairs={{0,8},{2,10},{4,12},{6,14},{8,0},{10,2},{12,4},{14,6},{1,9},{3,11}... | collective-permute-start | bytes 393224 | tf_op jit(solution)/shard_map/ppermute | solution.py:49
  553.0 10.5 %collective-permute-start.43 = (bf16[64,640]{1,0:T(8,128)(2,1)S(1)}, bf16[64,640]{1,0:T(8,128)(2,1)S(1)}, u32[]{:S(2)}, u32[]{:S(2)}) collective-permute-start(bf16[64,640]{1,0:T(8,128)(2,1)S(1)} %dynamic-slice_bitcast_fusion.11), channel_id=1, source_target_pairs={{0,8},{2,10},{4,12},{6,14},{8,0},{10,2},{12,4},{14,6},{1,9},{3,11}... | collective-permute-start | bytes 245768 | tf_op jit(solution)/shard_map/ppermute | solution.py:49
  558.3 7.4 %collective-permute-start.46 = (bf16[2,64,768]{2,1,0:T(8,128)(2,1)S(1)}, bf16[2,64,768]{2,1,0:T(8,128)(2,1)S(1)}, u32[]{:S(2)}, u32[]{:S(2)}) collective-permute-start(bf16[2,64,768]{2,1,0:T(8,128)(2,1)S(1)} %dynamic-slice_bitcast_fusion.6), channel_id=1, source_target_pairs={{0,4},{2,6},{4,0},{6,2},{8,12},{10,14},{12,8},{14,10},{1,5},{3,7},... | collective-permute-start | bytes 589832 | tf_op jit(solution)/shard_map/ppermute | solution.py:49
  565.8 6.6 %collective-permute-start.47 = (bf16[64,768]{1,0:T(8,128)(2,1)S(1)}, bf16[64,768]{1,0:T(8,128)(2,1)S(1)}, u32[]{:S(2)}, u32[]{:S(2)}) collective-permute-start(bf16[64,768]{1,0:T(8,128)(2,1)S(1)} %dynamic-slice_bitcast_fusion.10), channel_id=1, source_target_pairs={{0,8},{2,10},{4,12},{6,14},{8,0},{10,2},{12,4},{14,6},{1,9},{3,11}... | collective-permute-start | bytes 294920 | tf_op jit(solution)/shard_map/ppermute | solution.py:49
  (76 other events, 448.1 us)
Sparse Core Ops, SparseCore 0:
  11.3 107.7 all-gather.2
  121.8 111.9 all-gather.4
  347.9 186.7 reduce-scatter.1
